TPU v7x, 32 devices: a whole 2x2x4 slice. The times are simulated.
32 devices in a mesh: blk: 4 (over y, x), ulys: 8 (over z, core).
Axes of the slice: x: 2, y: 2, z: 4, core: 2. Of those that a mesh axis runs over, the one named last changes fastest.
Arguments:
- mamba_input: bfloat16 [8192, 16384], P(('blk', 'ulys')), may hold values from -6 to 6
- gate_input: bfloat16 [8192, 16384], P(('blk', 'ulys')), may hold values from -6 to 6
- delta_low: bfloat16 [8192, 512], P(('blk', 'ulys')), may hold values from -12 to 12
- state_mixers: bfloat16 [8192, 32], P(('blk', 'ulys')), may hold values from -6 to 6
- conv_weight: bfloat16 [4, 16384], P(None, 'ulys'), may hold values from -3 to 3
- conv_bias: float32 [16384], P('ulys'), may hold values from -3 to 3
- delta_weight: bfloat16 [512, 16384], P(None, 'ulys'), may hold values from -0.25 to 0.25
- delta_bias: float32 [16384], P('ulys'), may hold values from -12 to -2.3
- decay_log: float32 [16, 16384], P(None, 'ulys'), may hold values from -1 to 2.7
- skip_gain: float32 [16384], P('ulys'), may hold values from 0.5 to 1.5
- queries: bfloat16 [8192, 4096], P(('blk', 'ulys')), may hold values from -4.5 to 4.5
- key_rows: bfloat16 [8192, 1024], P(('blk', 'ulys')), may hold values from -4.5 to 4.5
- value_rows: bfloat16 [8192, 1024], P(('blk', 'ulys')), may hold values from -6 to 6
- span_order: int32 [8], replicated, may hold values from 0 to 7, as said below
Outputs:
- mamba_output: bfloat16 [8192, 16384], P(('blk', 'ulys'))
- attention_output: bfloat16 [8192, 4096], P(('blk', 'ulys'))
Inputs may be any that keep to these rules, and one draw needn't show every extreme that they name: `span_order`: device i of blk holds stored blocks 2i and 2i+1, whose sequence places are p and 7 - p for some p below 4, in either order; every sequence place appears once; the device holding places 0 and 7 and the device holding places 1 and 6 are 2 apart along blk.
All inputs are finite; a program needn't handle non-finite values.
Results may differ from a plain program's by a relative error of at most 0.013.
Values may be sent and summed in bfloat16 or wider, within the bound.
No kernel may reach another device: no remote copies, remote signals or barrier semaphores. Data moves between devices by JAX's collectives and lax.ppermute only.
A program may use at most 192 MiB of HBM per device.

v0:
```python
import functools

import jax
import jax.numpy as jnp
from jax import lax
from jax.experimental import pallas as pl
from jax.experimental.pallas import tpu as pltpu
from jax.sharding import Mesh
from jax.sharding import PartitionSpec as P


STATE = 16
CONV = 4
HD = 128
SPAN = 1024
LANES = 128
PAIR = 2
GROUP = 16
PIECES = 2
ONES = 16
NEG_LARGE = -1e30
LOG2E = 1.4426950408889634
PARAM_ROWS = 24
VMEM_LIMIT = 56 * 1024 * 1024


def softplus(x):
    return jnp.maximum(x, 0.0) + jnp.log1p(jnp.exp(-jnp.abs(x)))


def silu(x):
    half = 0.5 * x
    return half * jnp.tanh(half) + half


def lane_tiles(cols):
    size = min(LANES, cols)
    return [slice(at, at + size) for at in range(0, cols, size)]


def spread(ref, k, row, count):
    return jnp.broadcast_to(ref[k, pl.ds(row, 1), :], (count, ref.shape[2]))


def scan_kernel(
    core_ref, own_ref, other_ref, halo_ref, low_own_ref, low_other_ref, param_ref, inject_ref,
    read_ref, *refs, sources,
):
    weight_refs = refs[:sources]
    delta_ref, y_ref, sent_ref = refs[sources : sources + 3]
    x_scr, driven_scr, push_scr, hist_scr, rate_scr, param_scr = refs[sources + 3 :]
    core = core_ref[0]
    tokens, cols = y_ref.shape
    half = tokens // 2
    depth = low_own_ref.shape[1]
    tiles = lane_tiles(cols)
    mine = pl.multiple_of(core * half, 8)
    theirs = pl.multiple_of((1 - core) * half, 8)
    weight = jnp.concatenate(
        [ref[...].reshape(depth // sources, cols) for ref in weight_refs], axis=0
    )
    raw_mine = jnp.dot(low_own_ref[...], weight, preferred_element_type=jnp.float32)
    for k, tile in enumerate(tiles):
        delta_ref[k, pl.ds(mine, half), :] = raw_mine[:, tile]
    raw_theirs = jnp.dot(low_other_ref[...], weight, preferred_element_type=jnp.float32)
    for k, tile in enumerate(tiles):
        delta_ref[k, pl.ds(theirs, half), :] = raw_theirs[:, tile]
    for k, tile in enumerate(tiles):
        x_scr[k, 0:8, :] = halo_ref[:, tile].astype(jnp.float32)
        x_scr[k, pl.ds(8 + mine, half), :] = own_ref[:, tile].astype(jnp.float32)
        x_scr[k, pl.ds(8 + theirs, half), :] = other_ref[:, tile].astype(jnp.float32)
    rate_scr[...] = -LOG2E * jnp.exp(param_ref[0, :STATE, :])
    for k in range(CONV + 3):
        param_scr[8 * k : 8 * k + 8, :] = jnp.broadcast_to(
            param_ref[0, STATE + k : STATE + k + 1, :], (8, cols)
        )

    def prepare(step, total):
        first = pl.multiple_of(step * 8, 8)
        total = list(total)
        for k, tile in enumerate(tiles):
            mixed = param_scr[8 * CONV : 8 * CONV + 8, tile]
            for j in range(CONV):
                shifted = x_scr[k, pl.ds(first + 8 - (CONV - 1) + j, 8), :]
                mixed = mixed + param_scr[8 * j : 8 * j + 8, tile] * shifted
            driven = silu(mixed)
            delta = softplus(
                delta_ref[k, pl.ds(first, 8), :] + param_scr[8 * CONV + 8 : 8 * CONV + 16, tile]
            )
            delta_ref[k, pl.ds(first, 8), :] = delta
            driven_scr[pl.ds(first, 8), tile] = driven * param_scr[8 * CONV + 16 : 8 * CONV + 24, tile]
            push_scr[k, pl.ds(first, 8), :] = driven * delta
            total[k] = total[k] + delta
        return tuple(total)

    zero = jnp.zeros((8, tiles[0].stop), jnp.float32)
    total = lax.fori_loop(0, tokens // 8, prepare, (zero,) * len(tiles))
    total = jnp.sum(jnp.concatenate(total, axis=1), axis=0, keepdims=True)

    def step16(group, hidden):
        base = pl.multiple_of(group * GROUP, GROUP)
        hidden = list(hidden)
        for i in range(GROUP):
            inject = inject_ref[pl.ds(pl.multiple_of((base + i) * STATE, STATE), STATE), :]
            for k, tile in enumerate(tiles):
                decay = jnp.exp2(spread(delta_ref, k, base + i, STATE) * rate_scr[:, tile])
                push = spread(push_scr, k, base + i, STATE)
                hidden[k] = decay * hidden[k] + push * inject
            hist_scr[i * STATE : (i + 1) * STATE, :] = jnp.concatenate(hidden, axis=1).astype(
                jnp.bfloat16
            )
        read = read_ref[pl.ds(base, GROUP), :]
        out = jnp.dot(read, hist_scr[...], preferred_element_type=jnp.float32)
        y_ref[pl.ds(base, GROUP), :] = (out + driven_scr[pl.ds(base, GROUP), :]).astype(y_ref.dtype)
        return tuple(hidden)

    zero = jnp.zeros((STATE, tiles[0].stop), jnp.float32)
    end = lax.fori_loop(0, tokens // GROUP, step16, (zero,) * len(tiles))
    end = jnp.concatenate(end, axis=1)
    top = total.astype(jnp.bfloat16).astype(jnp.float32)
    mid = (total - top).astype(jnp.bfloat16).astype(jnp.float32)
    low = total - top - mid
    row = lax.broadcasted_iota(jnp.int32, (STATE, cols), 0)
    rows = jnp.where(row == 0, top, jnp.where(row == 1, mid, jnp.where(row == 2, low, 0.0)))
    share = sent_ref.shape[2]
    for k in range(sent_ref.shape[0]):
        at = slice(k * share, (k + 1) * share)
        sent_ref[k, :STATE, :] = end[:, at].astype(sent_ref.dtype)
        sent_ref[k, STATE:, :] = rows[:, at].astype(sent_ref.dtype)


def correct_body(
    core_ref, delta_ref, y_ref, enter_ref, param_ref, read_ref, own_gate_ref, other_gate_ref,
    mine_ref, theirs_ref, hist_scr, out_scr, rate_scr, enter_scr,
):
    core = core_ref[0]
    enter_scr[...] = jnp.concatenate([enter_ref[k] for k in range(enter_ref.shape[0])], axis=1)
    tokens, cols = y_ref.shape
    half = tokens // 2
    rate_scr[...] = -LOG2E * jnp.exp(param_ref[0, :STATE, :])

    tiles = lane_tiles(cols)

    def step16(group, elapsed):
        base = pl.multiple_of(group * GROUP, GROUP)
        elapsed = list(elapsed)
        for i in range(GROUP):
            carried = []
            for k, tile in enumerate(tiles):
                elapsed[k] = elapsed[k] + spread(delta_ref, k, base + i, 8)
                twice = jnp.concatenate([elapsed[k], elapsed[k]], axis=0)
                carried.append(jnp.exp2(twice * rate_scr[:, tile]))
            carried = jnp.concatenate(carried, axis=1).astype(jnp.bfloat16)
            hist_scr[i * STATE : (i + 1) * STATE, :] = carried * enter_scr[...]
        read = read_ref[pl.ds(base, GROUP), :]
        out = jnp.dot(read, hist_scr[...], preferred_element_type=jnp.float32)
        total = out + y_ref[pl.ds(base, GROUP), :].astype(jnp.float32)
        out_scr[pl.ds(base, GROUP), :] = total.astype(jnp.bfloat16).astype(jnp.float32)
        return tuple(elapsed)

    zero = jnp.zeros((8, tiles[0].stop), jnp.float32)
    lax.fori_loop(0, tokens // GROUP, step16, (zero,) * len(tiles))
    rows = 16

    def gated(gate_ref, dest_ref, offset):
        def body(step, carry):
            first = pl.multiple_of(step * rows, rows)
            gate = gate_ref[pl.ds(first, rows), :].astype(jnp.float32)
            value = out_scr[pl.ds(pl.multiple_of(offset + first, 8), rows), :]
            dest_ref[pl.ds(first, rows), :] = (value * silu(gate)).astype(dest_ref.dtype)
            return carry

        lax.fori_loop(0, half // rows, body, 0)

    gated(own_gate_ref, mine_ref, core * half)
    gated(other_gate_ref, theirs_ref, (1 - core) * half)


def correct_kernel(core_ref, *refs, resumed):
    correct_body(core_ref, *(refs[1:] if resumed else refs))


def combine_kernel(order_ref, got_ref, rate_ref, enter_ref):
    chunks = got_ref.shape[0]
    rates = rate_ref[...]

    def body(place, state):
        chunk = order_ref[place]
        enter_ref[chunk] = state.astype(enter_ref.dtype)
        got = got_ref[chunk].astype(jnp.float32)
        total = got[STATE : STATE + 1] + got[STATE + 1 : STATE + 2] + got[STATE + 2 : STATE + 3]
        return jnp.exp2(total * rates) * state + got[:STATE]

    lax.fori_loop(0, chunks, body, jnp.zeros(rates.shape, jnp.float32))


def copy_kernel(core_ref, in_ref, out_ref):
    out_ref[...] = in_ref[...]


def place_kernel(core_ref, buffer_ref, in_ref, out_ref):
    out_ref[...] = in_ref[...]


def flash_kernel(
    side_ref, flip_ref, half_ref, diag_ref, first_ref, last_ref, q_ref, *refs, heads, rows, sources,
):
    kv_refs = refs[:sources]
    out_ref, query_scr, key_scr, value_scr, max_scr, acc_scr = refs[sources:]
    step = pl.program_id(0)
    scale = LOG2E * HD ** (-0.5)
    wide = 2 * HD
    span = q_ref.shape[0]

    for source in range(sources):

        @pl.when(flip_ref[step] == source)
        def _(kv_ref=kv_refs[source]):
            key_scr[:, :HD] = kv_ref[:, :HD]
            key_scr[:, HD:] = kv_ref[:, :HD]
            value_scr[:HD, :] = kv_ref[:, HD:].T

    value_scr[HD:, :] = jnp.ones((ONES, span), jnp.bfloat16)

    @pl.when(first_ref[step] == 1)
    def _():
        max_scr[...] = jnp.full(max_scr.shape, NEG_LARGE, jnp.float32)
        acc_scr[...] = jnp.zeros(acc_scr.shape, jnp.float32)
        for head in range(heads):
            scaled = q_ref[:, head * HD : (head + 1) * HD].astype(jnp.float32) * scale
            coarse = scaled.astype(jnp.bfloat16)
            query_scr[:, head * wide : head * wide + HD] = coarse
            query_scr[:, head * wide + HD : (head + 1) * wide] = (
                scaled - coarse.astype(jnp.float32)
            ).astype(jnp.bfloat16)

    def score(head, row, key_count, masked):
        q = query_scr[row : row + rows, head * wide : (head + 1) * wide]
        scores = lax.dot_general(
            key_scr[:key_count, :], q, (((1,), (1,)), ((), ())),
            preferred_element_type=jnp.float32,
        )
        if masked:
            last = scores[row:, :]
            key_at = lax.broadcasted_iota(jnp.int32, last.shape, 0)
            query_at = lax.broadcasted_iota(jnp.int32, last.shape, 1)
            last = jnp.where(key_at <= query_at, last, NEG_LARGE)
            scores = jnp.concatenate([scores[:row, :], last], axis=0) if row else last
        return scores

    def absorb(head, row, key_count, scores):
        at = slice(row, row + rows)
        old_max = max_scr[head, 0:1, at]
        new_max = jnp.maximum(old_max, jnp.max(scores, axis=0, keepdims=True))
        weights = jnp.exp2(scores - new_max).astype(jnp.bfloat16)
        shrink = jnp.exp2(old_max - new_max)
        acc_scr[head, :, at] = acc_scr[head, :, at] * shrink + jnp.dot(
            value_scr[:, :key_count], weights, preferred_element_type=jnp.float32
        )
        max_scr[head, :, at] = jnp.broadcast_to(new_max, (8, rows))

    def sweep(masked):
        work = [(head, row) for head in range(heads) for row in range(0, span, rows)]
        count = [row + rows if masked else span for _, row in work]
        ahead = score(*work[0], count[0], masked)
        for i, (head, row) in enumerate(work):
            scores = ahead
            if i + 1 < len(work):
                ahead = score(*work[i + 1], count[i + 1], masked)
            absorb(head, row, count[i], scores)

    @pl.when(diag_ref[step] == 0)
    def _():
        sweep(False)

    @pl.when(diag_ref[step] == 1)
    def _():
        sweep(True)

    @pl.when(last_ref[step] == 1)
    def _():
        for head in range(heads):
            for row in range(0, span, rows):
                at = slice(row, row + rows)
                ratio = acc_scr[head, :HD, at] / acc_scr[head, HD : HD + 1, at]
                out_ref[at, head * HD : (head + 1) * HD] = ratio.T.astype(out_ref.dtype)


def whole(shape):
    return pl.BlockSpec(
        shape, lambda j, core_ref: (0,) * len(shape), pipeline_mode=pl.Buffered(1)
    )


def shard_map_of(side, piece, first=0):
    return lambda j, core_ref: (
        0, (PAIR * (j + first) + (core_ref[0] + side) % PAIR) * PIECES + piece,
    )


def param_spec(count, width, piece, first):
    return pl.BlockSpec(
        (1, PARAM_ROWS, width),
        lambda j, core_ref: (lax.rem(core_ref[1] + count - (j + first), count), 0, piece),
    )


def plain(j, core_ref):
    return (0, j)


def run_pick(core, full, piece, width):
    half, inner = full.shape
    blocks = inner // (width * PIECES * PAIR)
    return pl.pallas_call(
        copy_kernel,
        grid_spec=pltpu.PrefetchScalarGridSpec(
            num_scalar_prefetch=1,
            grid=(blocks,),
            in_specs=[pl.BlockSpec((half, width), shard_map_of(1, piece))],
            out_specs=pl.BlockSpec((half, width), plain),
        ),
        out_shape=jax.ShapeDtypeStruct((half, blocks * width), full.dtype),
        name="pick_channels",
    )(core, full)


def run_place(core, full, part, piece, width, first):
    half, _ = full.shape
    blocks = part.shape[1] // width
    return pl.pallas_call(
        place_kernel,
        grid_spec=pltpu.PrefetchScalarGridSpec(
            num_scalar_prefetch=1,
            grid=(blocks,),
            in_specs=[pl.BlockSpec(memory_space=pl.ANY), pl.BlockSpec((half, width), plain)],
            out_specs=pl.BlockSpec((half, width), shard_map_of(1, piece, first)),
        ),
        out_shape=jax.ShapeDtypeStruct(full.shape, full.dtype),
        input_output_aliases={1: 0},
        name="place_channels",
    )(core, full, part)


def weight_spec(weight, width, shards, first):
    if weight.ndim == 4:
        parts, _, rows, _ = weight.shape
        return pl.BlockSpec((parts, 1, rows, width), lambda j, core_ref: (0, j + first, 0, 0))
    return pl.BlockSpec(
        (1, weight.shape[1], width),
        lambda j, core_ref: (lax.rem(core_ref[1] + shards - (j + first), shards), 0, 0),
    )


def run_scan(
    core, x_own, x_other, halo, low_own, low_other, weights, params, inject, read, piece, width, share,
    first, blocks,
):
    half = x_other.shape[0]
    cols = blocks * width
    tokens = 2 * half
    shards = params.shape[0]
    sources = len(weights)

    def shifted(j, core_ref):
        return (0, j + first)

    lanes = min(LANES, width)
    tiles = width // lanes
    return pl.pallas_call(
        functools.partial(scan_kernel, sources=sources),
        grid_spec=pltpu.PrefetchScalarGridSpec(
            num_scalar_prefetch=1,
            grid=(blocks,),
            in_specs=[
                pl.BlockSpec((half, width), shard_map_of(0, piece, first)),
                pl.BlockSpec((half, width), shifted),
                pl.BlockSpec((8, width), lambda j, core_ref: (0, piece * shards + j + first)),
                whole(low_own.shape),
                whole(low_other.shape),
                param_spec(shards, width, piece, first),
                whole(inject.shape),
                whole(read.shape),
            ]
            + [weight_spec(weight, width, shards, first) for weight in weights],
            out_specs=[
                pl.BlockSpec((tiles, tokens, lanes), lambda j, core_ref: (j, 0, 0)),
                pl.BlockSpec((tokens, width), plain),
                pl.BlockSpec((width // share, 2 * STATE, share), lambda j, core_ref: (j, 0, 0)),
            ],
            scratch_shapes=[
                pltpu.VMEM((tiles, tokens + 8, lanes), jnp.float32),
                pltpu.VMEM((tokens, width), jnp.float32),
                pltpu.VMEM((tiles, tokens, lanes), jnp.float32),
                pltpu.VMEM((GROUP * STATE, width), jnp.bfloat16),
                pltpu.VMEM((STATE, width), jnp.float32),
                pltpu.VMEM((8 * (CONV + 3), width), jnp.float32),
            ],
        ),
        out_shape=[
            jax.ShapeDtypeStruct((cols // lanes, tokens, lanes), jnp.float32),
            jax.ShapeDtypeStruct((tokens, cols), jnp.bfloat16),
            jax.ShapeDtypeStruct((cols // share, 2 * STATE, share), jnp.bfloat16),
        ],
        compiler_params=pltpu.CompilerParams(vmem_limit_bytes=VMEM_LIMIT),
        name="token_scan",
    )(core, x_own, x_other, halo, low_own, low_other, params, inject, read, *weights)


def run_correct(
    core, full, delta, y, enter, params, read, gate_own, gate_other, piece, width, first, inside, blocks
):
    tokens = y.shape[0]
    half, inner = gate_own.shape
    cols = blocks * width
    lanes = delta.shape[2]
    tiles = width // lanes
    share = enter.shape[2]
    resumed = full is not None
    first_spec = [pl.BlockSpec(memory_space=pl.ANY)] if resumed else []
    first_arg = (full,) if resumed else ()
    return pl.pallas_call(
        functools.partial(correct_kernel, resumed=resumed),
        grid_spec=pltpu.PrefetchScalarGridSpec(
            num_scalar_prefetch=1,
            grid=(blocks,),
            in_specs=first_spec
            + [
                pl.BlockSpec((tiles, tokens, lanes), lambda j, core_ref: (j + inside, 0, 0)),
                pl.BlockSpec((tokens, width), lambda j, core_ref: (0, j + inside)),
                pl.BlockSpec((width // share, STATE, share), lambda j, core_ref: (j + first, 0, 0)),
                param_spec(params.shape[0], width, piece, first),
                whole(read.shape),
                pl.BlockSpec((half, width), shard_map_of(0, piece, first)),
                pl.BlockSpec((half, width), lambda j, core_ref: (0, j + first)),
            ],
            out_specs=[
                pl.BlockSpec((half, width), shard_map_of(0, piece, first)),
                pl.BlockSpec((half, width), plain),
            ],
            scratch_shapes=[
                pltpu.VMEM((GROUP * STATE, width), jnp.bfloat16),
                pltpu.VMEM((tokens, width), jnp.float32),
                pltpu.VMEM((STATE, width), jnp.float32),
                pltpu.VMEM((STATE, width), jnp.bfloat16),
            ],
        ),
        out_shape=[
            jax.ShapeDtypeStruct((half, inner), jnp.bfloat16),
            jax.ShapeDtypeStruct((half, cols), jnp.bfloat16),
        ],
        input_output_aliases={1: 0} if resumed else {},
        compiler_params=pltpu.CompilerParams(vmem_limit_bytes=VMEM_LIMIT),
        name="state_correction",
    )(core, *first_arg, delta, y, enter, params, read, gate_own, gate_other)


def run_combine(order, got, rates):
    chunks, _, cols = got.shape
    return pl.pallas_call(
        combine_kernel,
        grid_spec=pltpu.PrefetchScalarGridSpec(
            num_scalar_prefetch=1,
            grid=(1,),
            in_specs=[
                pl.BlockSpec(got.shape, lambda i, o: (0, 0, 0)),
                pl.BlockSpec(rates.shape, lambda i, o: (0, 0)),
            ],
            out_specs=pl.BlockSpec((chunks, STATE, cols), lambda i, o: (0, 0, 0)),
        ),
        out_shape=jax.ShapeDtypeStruct((chunks, STATE, cols), jnp.bfloat16),
        compiler_params=pltpu.CompilerParams(vmem_limit_bytes=VMEM_LIMIT),
        name="state_combine",
    )(order, got, rates)


def run_flash(tables, q, kv_parts, rows=512):
    _, width = q.shape
    heads = width // HD
    steps = tables[0].shape[0]
    sources = len(kv_parts)

    def q_map(s, side, flip, half, diag, first, last):
        return (side[s], 0)

    def kv_map(s, side, flip, half, diag, first, last):
        return (half[s], 0)

    return pl.pallas_call(
        functools.partial(flash_kernel, heads=heads, rows=rows, sources=sources),
        grid_spec=pltpu.PrefetchScalarGridSpec(
            num_scalar_prefetch=6,
            grid=(steps,),
            in_specs=[pl.BlockSpec((SPAN, width), q_map)]
            + [pl.BlockSpec((SPAN, 2 * HD), kv_map)] * sources,
            out_specs=pl.BlockSpec((SPAN, width), q_map),
            scratch_shapes=[
                pltpu.VMEM((SPAN, 2 * width), jnp.bfloat16),
                pltpu.VMEM((SPAN, 2 * HD), jnp.bfloat16),
                pltpu.VMEM((HD + ONES, SPAN), jnp.bfloat16),
                pltpu.VMEM((heads, 8, SPAN), jnp.float32),
                pltpu.VMEM((heads, HD + ONES, SPAN), jnp.float32),
            ],
        ),
        out_shape=jax.ShapeDtypeStruct(q.shape, jnp.bfloat16),
        compiler_params=pltpu.CompilerParams(vmem_limit_bytes=VMEM_LIMIT),
        name="causal_attention",
    )(*tables, q, *kv_parts)


def flash_tables(span_order, my_blocks, blk):
    block_total = span_order.shape[0]
    places = jnp.arange(block_total, dtype=jnp.int32)
    holder = jnp.sum(jnp.where(span_order[None, :] == places[:, None], places[None, :], 0), axis=1)
    steps = jnp.arange(block_total + 1, dtype=jnp.int32)
    first_count = my_blocks[0] + 1
    side = (steps >= first_count).astype(jnp.int32)
    place = jnp.where(side == 1, steps - first_count, steps)
    limit = jnp.where(side == 1, my_blocks[1], my_blocks[0])
    block = jnp.sum(jnp.where(places[None, :] == place[:, None], holder[None, :], 0), axis=1)
    block = block.astype(jnp.int32)
    last = (place == limit).astype(jnp.int32)
    first = (place == 0).astype(jnp.int32)
    return (side, (block // 2) ^ blk.astype(jnp.int32), block % 2, last, first, last)


def local(
    mamba_input, gate_input, delta_low, state_mixers, conv_weight, conv_bias, delta_weight,
    delta_bias, decay_log, skip_gain, queries, key_rows, value_rows, span_order,
):
    blk = lax.axis_index("blk")
    chip = lax.axis_index("chip")
    core = lax.axis_index("core")
    blk_count = lax.axis_size("blk")
    chip_count = lax.axis_size("chip")
    ulys = ("chip", "core")
    chips = ("blk", "chip")
    ulys_count = chip_count * PAIR
    chunks = blk_count * chip_count
    block_total = span_order.shape[0]
    half, _ = mamba_input.shape
    tokens = PAIR * half
    shard_cols = delta_weight.shape[1]
    width = shard_cols // PIECES
    cols = chip_count * width
    swap = [(0, 1), (1, 0)]
    core_arr = jnp.stack([core, chip]).astype(jnp.int32)
    my_blocks = lax.dynamic_slice_in_dim(span_order, 2 * blk, 2, 0)

    depth = delta_weight.shape[0]
    part_rows = depth // blk_count
    part = lax.dynamic_slice_in_dim(delta_weight, blk * part_rows, part_rows, 0)
    far_moves = [
        [(i, (i + far) % chip_count) for i in range(chip_count)] for far in range(1, chip_count)
    ]
    flips = [[(i, i ^ flip) for i in range(blk_count)] for flip in range(1, blk_count)]
    part_first, part_later = part[:, :width], part[:, width:]
    shards_first = jnp.stack(
        [part_first] + [lax.ppermute(part_first, "chip", move) for move in far_moves]
    )
    weights_first = [shards_first] + [
        lax.ppermute(shards_first, "blk", move) for move in flips
    ]
    weights_later = lax.all_gather(part_later, chips, axis=0, tiled=False)
    weights_later = [weights_later.reshape(blk_count, chip_count, part_rows, width)]

    def by_flip(low):
        return jnp.concatenate(
            [
                lax.dynamic_slice_in_dim(low, (blk ^ flip) * part_rows, part_rows, 1)
                for flip in range(blk_count)
            ],
            axis=1,
        )

    kv_heads = key_rows.shape[1] // HD
    repeat = ulys_count // kv_heads
    kv_rows = jnp.stack(
        [key_rows.reshape(half, kv_heads, HD), value_rows.reshape(half, kv_heads, HD)], axis=2
    )
    kv_rows = jnp.broadcast_to(
        kv_rows[:, :, None], (half, kv_heads, repeat, 2, HD)
    ).reshape(half, ulys_count * 2 * HD)
    kv_rows, _ = lax.optimization_barrier((kv_rows, shards_first))
    kv_local = lax.all_to_all(kv_rows, ulys, split_axis=1, concat_axis=0, tiled=True)

    packed = jnp.concatenate(
        [
            decay_log,
            conv_weight.astype(jnp.float32),
            conv_bias[None],
            delta_bias[None],
            skip_gain[None],
            jnp.zeros((1, shard_cols), jnp.float32),
        ],
        axis=0,
    )
    x_other = [
        lax.ppermute(run_pick(core_arr, mamba_input, piece, width), "core", swap)
        for piece in range(PIECES)
    ]
    low_other = lax.ppermute(delta_low, "core", swap)
    mixers_other = lax.ppermute(state_mixers, "core", swap)
    mixers = jnp.where(
        core == 0,
        jnp.concatenate([state_mixers, mixers_other], axis=0),
        jnp.concatenate([mixers_other, state_mixers], axis=0),
    )
    inject = jnp.broadcast_to(
        mixers[:, :STATE].astype(jnp.float32).reshape(tokens * STATE, 1), (tokens * STATE, LANES)
    )
    same = jnp.arange(tokens, dtype=jnp.int32)[:, None] % GROUP == jnp.arange(GROUP, dtype=jnp.int32)
    read = jnp.where(
        same[:, :, None], mixers[:, None, STATE:], jnp.zeros((), jnp.bfloat16)
    ).reshape(tokens, GROUP * STATE)

    per_block = SPAN // tokens
    chunk_ids = jnp.arange(chunks, dtype=jnp.int32)
    stored = chunk_ids // per_block
    block_ids = jnp.arange(block_total, dtype=jnp.int32)
    block_pos = jnp.sum(
        jnp.where(stored[:, None] == block_ids[None, :], span_order[None, :], 0), axis=1
    )
    chunk_pos = block_pos * per_block + chunk_ids % per_block
    order = jnp.sum(
        jnp.where(chunk_pos[None, :] == chunk_ids[:, None], chunk_ids[None, :], 0), axis=1
    ).astype(jnp.int32)
    me = blk * chip_count + chip
    my_pos = jnp.sum(jnp.where(chunk_ids == me, chunk_pos, 0))
    own_tail = lax.dynamic_index_in_dim(
        mamba_input[half - (CONV - 1) :].reshape(CONV - 1, chip_count, PAIR, PIECES, width),
        core, 2, False,
    ).swapaxes(1, 2).reshape(CONV - 1, PIECES * cols)
    other_tail = jnp.concatenate([x[half - (CONV - 1) :] for x in x_other], axis=1)
    tail = jnp.where(core == 1, own_tail, other_tail)
    gate_other = [
        lax.ppermute(run_pick(core_arr, gate_input, piece, width), "core", swap)
        for piece in range(PIECES)
    ]

    params = jnp.stack([packed] + [lax.ppermute(packed, "chip", move) for move in far_moves])

    kv_local, tail = lax.optimization_barrier((kv_local, tail))
    tails = lax.all_to_all(
        jnp.broadcast_to(tail[None], (chunks, CONV - 1, PIECES * cols)), chips,
        split_axis=0, concat_axis=0, tiled=True,
    )
    before = (chunk_pos == my_pos - 1).astype(jnp.bfloat16)
    halo = jnp.einsum("m,mkc->kc", before, tails, preferred_element_type=jnp.float32)
    halo = jnp.concatenate(
        [jnp.zeros((8 - (CONV - 1), PIECES * cols), jnp.bfloat16), halo.astype(jnp.bfloat16)],
        axis=0,
    )

    share = cols // chunks
    split = chip_count // 2

    def scan_part(piece, x_piece, lows, weights, first, blocks):
        return run_scan(
            core_arr, mamba_input, x_piece, halo, *lows, weights, params, inject, read, piece,
            width, share, first, blocks,
        )

    def rates_of(piece):
        at = me * share
        shard = at // width
        far = (chip + chip_count - shard) % chip_count
        mine = lax.dynamic_slice(
            params, (far, 0, piece * width + at % width), (1, STATE, share)
        )
        return -LOG2E * jnp.exp(mine[0])

    my_rates = [rates_of(piece) for piece in range(PIECES)]

    def to_owners(array):
        return lax.all_to_all(array, chips, split_axis=0, concat_axis=0, tiled=True)

    def correct_part(full, made, enter, piece, first, inside, blocks):
        delta, y = made[:2]
        return run_correct(
            core_arr, full, delta, y, enter, params, read, gate_input, gate_other[piece], piece,
            width, first, inside, blocks,
        )

    lows_first = (by_flip(delta_low), by_flip(low_other))
    lows_later = (delta_low, low_other)
    tables = flash_tables(span_order, my_blocks, blk)
    x_now, gate_other, my_rates, tables, order = lax.optimization_barrier(
        (x_other[0], gate_other, my_rates, tables, order)
    )
    made_0 = scan_part(0, x_now, lows_first, weights_first, 0, chip_count)
    halo, queries, kv_local = lax.optimization_barrier((halo, queries, kv_local))
    q_local = lax.all_to_all(queries, ulys, split_axis=1, concat_axis=0, tiled=True)
    kv_parts = [kv_local] + [lax.ppermute(kv_local, "blk", move) for move in flips]
    x_now, sent_0, q_local, kv_parts, my_rates = lax.optimization_barrier(
        (x_other[1], made_0[2], q_local, kv_parts, my_rates)
    )
    got_0 = to_owners(sent_0)
    made_1a = scan_part(1, x_now, lows_later, weights_later, 0, split)
    x_now, got_0, sent_1a = lax.optimization_barrier((x_now, got_0, made_1a[2]))
    enter_0 = to_owners(run_combine(order, got_0, my_rates[0]))
    made_1b = scan_part(1, x_now, lows_later, weights_later, split, chip_count - split)
    enter_0, sent_1, q_local = lax.optimization_barrier(
        (enter_0, jnp.concatenate([sent_1a, made_1b[2]], axis=0), q_local)
    )
    got_1 = to_owners(sent_1)
    attended = run_flash(tables, q_local, kv_parts)
    enter_0, got_1, attended = lax.optimization_barrier((enter_0, got_1, attended))
    enter_1 = to_owners(run_combine(order, got_1, my_rates[1]))
    full, theirs_0 = correct_part(None, made_0, enter_0, 0, 0, 0, chip_count)
    full, enter_1, attended = lax.optimization_barrier((full, enter_1, attended))
    back_0 = lax.ppermute(theirs_0, "core", swap)
    attention_output = lax.all_to_all(attended, ulys, split_axis=0, concat_axis=1, tiled=True)
    full, theirs_1a = correct_part(full, made_1a, enter_1, 1, 0, 0, split)
    back_1a = lax.ppermute(theirs_1a, "core", swap)
    full, theirs_1b = correct_part(full, made_1b, enter_1, 1, split, 0, chip_count - split)
    back_1b = lax.ppermute(theirs_1b, "core", swap)
    full = run_place(core_arr, full, back_0, 0, width, 0)
    full = run_place(core_arr, full, back_1a, 1, width, 0)
    mamba_output = run_place(core_arr, full, back_1b, 1, width, split)
    return (mamba_output, attention_output)


def solution(mesh):
    blk_count = mesh.shape["blk"]
    ulys_count = mesh.shape["ulys"]
    fine = Mesh(
        mesh.devices.reshape(blk_count, ulys_count // PAIR, PAIR), ("blk", "chip", "core")
    )
    rows = P(("blk", "chip", "core"), None)
    col = ("chip", "core")
    placed = (
        rows, rows, rows, rows,
        P(None, col), P(col), P(None, col), P(col), P(None, col), P(col),
        rows, rows, rows,
        P(),
    )

    return jax.shard_map(local, mesh=fine, in_specs=placed, out_specs=(rows, rows), check_vma=False)
```

profile of v0, /device:TPU:0, one launch (start us, length us, event | category | flops | bytes accessed | tf_op | source)
XLA Modules:
  0.0 602.2 jit_solution(5338116520107971227)
XLA Ops:
  7.2 1.8 fusion.12
  8.9 5.1 collective-permute-start.8
  14.0 1.0 collective-permute-start.6
  15.6 4.5 pick_channels.4
  20.0 4.6 pick_channels.7
  25.2 1.2 copy.38
  26.5 1.1 pad_maximum_fusion
  27.5 8.9 %collective-permute-done.7 = bf16[128,1024]{1,0:T(8,128)(2,1)} collective-permute-done((bf16[128,1024]{1,0:T(8,128)(2,1)S(1)}, bf16[128,1024]{1,0:T(8,128)(2,1)}, u32[]{:S(2)}, u32[]{:S(2)}) %collective-permute-start.7) | collective-permute-done | bytes 262176 | tf_op jit(solution)/shard_map/ppermute | solution.py:559
  36.4 2.2 pad_maximum_fusion.1.refs_0_
  38.7 4.1 all-to-all-start
  43.5 1.0 slice.31
  44.8 30.1 %all-to-all-done = bf16[256,8,256]{0,2,1:T(8,128)(2,1)S(1)} async-done(((bf16[256,8,256]{0,2,1:T(8,128)(2,1)}), bf16[256,8,256]{0,2,1:T(8,128)(2,1)S(1)}, u32[]{:S(2)}, u32[]{:S(2)}) %all-to-all-start) | async-done | bytes 1048608 | tf_op jit(solution)/shard_map/all_to_all | solution.py:585
  74.9 1.0 copy-done.4
  75.9 1.5 copy.40
  77.5 0.9 slice.37
  78.5 1.4 broadcast_in_dim.137
  79.8 4.3 all-to-all-start.1
  85.6 35.0 %all-to-all-done.1 = bf16[16,3,8192]{2,1,0:T(4,128)(2,1)} async-done(((bf16[16,3,8192]{2,1,0:T(4,128)(2,1)}), bf16[16,3,8192]{2,1,0:T(4,128)(2,1)}, u32[]{:S(2)}, u32[]{:S(2)}) %all-to-all-start.1) | async-done | bytes 786464 | tf_op jit(solution)/shard_map/all_to_all | solution.py:644
  120.6 2.2 fusion
  123.6 3.2 copy.60
  126.7 4.3 all-to-all-start.2
  131.1 4.5 pick_channels.5
  136.0 4.5 pick_channels.6
  140.6 2.1 concatenate.24
  142.7 3.7 collective-permute-start.5
  148.4 0.8 select_reduce_fusion.3
  151.2 1.3 select_reduce_fusion.order_ref
  152.5 25.4 %collective-permute-done.5 = f32[24,2048]{1,0:T(8,128)} collective-permute-done((f32[24,2048]{1,0:T(8,128)}, f32[24,2048]{1,0:T(8,128)}, u32[]{:S(2)}, u32[]{:S(2)}) %collective-permute-start.5) | collective-permute-done | bytes 196640 | tf_op jit(solution)/shard_map/ppermute | solution.py:641
  178.0 1.8 compare_convert_fusion
  179.8 19.4 %collective-permute-done.4 = f32[24,2048]{1,0:T(8,128)} collective-permute-done((f32[24,2048]{1,0:T(8,128)}, f32[24,2048]{1,0:T(8,128)}, u32[]{:S(2)}, u32[]{:S(2)}) %collective-permute-start.4) | collective-permute-done | bytes 196640 | tf_op jit(solution)/shard_map/ppermute | solution.py:641
  199.7 0.8 maximum_select_fusion.1
  200.5 7.6 %collective-permute-done.3 = f32[24,2048]{1,0:T(8,128)S(1)} collective-permute-done((f32[24,2048]{1,0:T(8,128)}, f32[24,2048]{1,0:T(8,128)S(1)}, u32[]{:S(2)}, u32[]{:S(2)}) %collective-permute-start.3) | collective-permute-done | bytes 196640 | tf_op jit(solution)/shard_map/ppermute | solution.py:641
  208.1 1.2 collective-permute-start.13
  209.3 0.9 collective-permute-start.14
  210.2 1.4 collective-permute-start.15
  211.6 1.2 collective-permute-start.16
  212.8 0.9 collective-permute-start.17
  214.4 0.9 copy.42
  216.8 0.9 copy.43.read_ref.refs_4_.refs_5_
  217.6 1.3 pad_maximum_fusion.2.param_ref.refs_3_.refs_4_
  219.7 1.0 constant_dynamic-slice_fusion.3
  220.6 0.9 pad_maximum_fusion.3
  221.5 37.6 %collective-permute-done.13.refs_2_ = bf16[4,128,1024]{2,1,0:T(8,128)(2,1)} collective-permute-done((bf16[4,128,1024]{2,1,0:T(8,128)(2,1)}, bf16[4,128,1024]{2,1,0:T(8,128)(2,1)}, u32[]{:S(2)}, u32[]{:S(2)}) %collective-permute-start.13) | collective-permute-done | bytes 1048608 | tf_op jit(solution)/shard_map/ppermute | solution.py:562
  259.1 2.6 broadcast_in_dim.140.inject_ref
  261.7 64.4 %token_scan.3 = (f32[32,512,128]{2,1,0:T(8,128)}, bf16[512,4096]{1,0:T(8,128)(2,1)}, bf16[16,32,256]{2,1,0:T(8,128)(2,1)}) custom-call(s32[2]{0:T(128)} %pad_add_fusion.core_ref, bf16[256,16384]{1,0:T(8,128)(2,1)} %own_ref.5, bf16[256,4096]{1,0:T(8,128)(2,1)} %collective-permute-done.other_ref, bf16[8,8192]{1,0:T(8,128)(2,1)} %concatenate.26.halo_ref, ...), custom_call_target="tpu_custom_call" | custom-call | tf_op jit(solution)/shard_map/token_scan/pallas_call | solution.py:370
  326.1 3.5 all-to-all-start.3
  329.7 34.8 %token_scan.4 = (f32[16,512,128]{2,1,0:T(8,128)}, bf16[512,2048]{1,0:T(8,128)(2,1)}, bf16[8,32,256]{2,1,0:T(8,128)(2,1)}) custom-call(s32[2]{0:T(128)} %pad_add_fusion.core_ref, bf16[256,16384]{1,0:T(8,128)(2,1)} %own_ref.5, bf16[256,4096]{1,0:T(8,128)(2,1)} %copy-done.1, bf16[8,8192]{1,0:T(8,128)(2,1)} %concatenate.26.halo_ref, ...), custom_call_target="tpu_custom_call" | custom-call | tf_op jit(solution)/shard_map/token_scan/pallas_call | solution.py:370
  365.2 2.5 state_combine.2
  367.7 6.9 %all-to-all-start.4 = ((bf16[16,16,256]{2,1,0:T(8,128)(2,1)}), bf16[16,16,256]{2,1,0:T(8,128)(2,1)S(1)}, u32[]{:S(2)}, u32[]{:S(2)}) async-start(bf16[16,16,256]{2,1,0:T(8,128)(2,1)} %state_combine.2), calls=%async_computation.4 | async-start | bytes 262144 | tf_op jit(solution)/shard_map/all_to_all | solution.py:676
  374.6 34.9 %token_scan.5 = (f32[16,512,128]{2,1,0:T(8,128)}, bf16[512,2048]{1,0:T(8,128)(2,1)}, bf16[8,32,256]{2,1,0:T(8,128)(2,1)}) custom-call(s32[2]{0:T(128)} %pad_add_fusion.core_ref, bf16[256,16384]{1,0:T(8,128)(2,1)} %own_ref.5, bf16[256,4096]{1,0:T(8,128)(2,1)} %copy-done.1, bf16[8,8192]{1,0:T(8,128)(2,1)} %concatenate.26.halo_ref, ...), custom_call_target="tpu_custom_call" | custom-call | tf_op jit(solution)/shard_map/token_scan/pallas_call | solution.py:370
  409.6 1.6 pad_maximum_fusion.5
  411.2 6.9 %all-to-all-start.5 = ((bf16[16,32,256]{2,1,0:T(8,128)(2,1)}), bf16[16,32,256]{2,1,0:T(8,128)(2,1)S(1)}, u32[]{:S(2)}, u32[]{:S(2)}) async-start(bf16[16,32,256]{2,1,0:T(8,128)(2,1)} %pad_maximum_fusion.5), calls=%async_computation.5 | async-start | bytes 524288 | tf_op jit(solution)/shard_map/all_to_all | solution.py:676
  418.1 58.2 %causal_attention.1 = bf16[2048,512]{1,0:T(8,128)(2,1)} custom-call(s32[9]{0:T(128)} %compare_convert_fusion.2.side_ref, s32[9]{0:T(128)} %get-tuple-element.81.flip_ref, s32[9]{0:T(128)} %get-tuple-element.82.half_ref, s32[9]{0:T(128)} %get-tuple-element.85.diag_ref.last_ref, s32[9]{0:T(128)} %get-tuple-element.84.first_ref, ...), custom_call_target="tpu_custom_call" | custom-call | tf_op jit(solution)/shard_map/causal_attention/pallas_call | solution.py:489
  477.0 2.5 state_combine.3
  479.6 6.9 %all-to-all-start.6 = ((bf16[16,16,256]{2,1,0:T(8,128)(2,1)}), bf16[16,16,256]{2,1,0:T(8,128)(2,1)S(1)}, u32[]{:S(2)}, u32[]{:S(2)}) async-start(bf16[16,16,256]{2,1,0:T(8,128)(2,1)} %state_combine.3), calls=%async_computation.6 | async-start | bytes 262144 | tf_op jit(solution)/shard_map/all_to_all | solution.py:676
  486.5 42.4 %state_correction.3 = (bf16[256,16384]{1,0:T(8,128)(2,1)}, bf16[256,4096]{1,0:T(8,128)(2,1)}) custom-call(s32[2]{0:T(128)} %pad_add_fusion.core_ref, f32[32,512,128]{2,1,0:T(8,128)} %get-tuple-element.59.refs_0_, bf16[512,4096]{1,0:T(8,128)(2,1)} %get-tuple-element.60.refs_1_, bf16[16,16,256]{2,1,0:T(8,128)(2,1)} %copy-done.10, f32[4,24,2048]{2,1,0:T(8,128)} %copy-done, ...), custom_call_target="tpu_custom_call" | custom-call | tf_op jit(solution)/shard_map/state_correction/pallas_call | solution.py:422
  529.6 5.0 all-to-all-start.7
  535.1 23.6 %state_correction.4 = (bf16[256,16384]{1,0:T(8,128)(2,1)}, bf16[256,2048]{1,0:T(8,128)(2,1)}) custom-call(s32[2]{0:T(128)} %pad_add_fusion.core_ref, bf16[256,16384]{1,0:T(8,128)(2,1)} %get-tuple-element.97.refs_0_, f32[16,512,128]{2,1,0:T(8,128)} %get-tuple-element.98.refs_1_, ...), custom_call_target="tpu_custom_call", output_to_operand_aliasing={{0}: (1, {})} | custom-call | tf_op jit(solution)/shard_map/state_correction/pallas_call | solution.py:422
  558.7 23.7 %state_correction.5 = (bf16[256,16384]{1,0:T(8,128)(2,1)}, bf16[256,2048]{1,0:T(8,128)(2,1)}) custom-call(s32[2]{0:T(128)} %pad_add_fusion.core_ref, bf16[256,16384]{1,0:T(8,128)(2,1)} %get-tuple-element.102.refs_0_, f32[16,512,128]{2,1,0:T(8,128)} %get-tuple-element.103.refs_1_, ...), custom_call_target="tpu_custom_call", output_to_operand_aliasing={{0}: (1, {})} | custom-call | tf_op jit(solution)/shard_map/state_correction/pallas_call | solution.py:422
  582.9 4.5 place_channels.3.buffer_ref
  587.4 1.0 copy-done.7
  588.4 2.7 place_channels.4.buffer_ref
  591.1 2.7 place_channels.5
  593.8 1.6 copy.54
  (105 shorter events, 14.3 us)
Async XLA Ops:
  8.9 18.6 %collective-permute-start.8 = (bf16[128,1024]{1,0:T(8,128)(2,1)S(1)}, bf16[128,1024]{1,0:T(8,128)(2,1)}, u32[]{:S(2)}, u32[]{:S(2)}) collective-permute-start(bf16[128,1024]{1,0:T(8,128)(2,1)S(1)} %get-tuple-element.113), channel_id=1, source_target_pairs={{0,6},{2,0},{4,2},{6,4},{1,7},{3,1},{5,3},{7,5},{8,14},{10,8},{12,... | collective-permute-start | bytes 786440 | tf_op jit(solution)/shard_map/ppermute | solution.py:559
  14.0 22.4 %collective-permute-start.7 = (bf16[128,1024]{1,0:T(8,128)(2,1)S(1)}, bf16[128,1024]{1,0:T(8,128)(2,1)}, u32[]{:S(2)}, u32[]{:S(2)}) collective-permute-start(bf16[128,1024]{1,0:T(8,128)(2,1)S(1)} %get-tuple-element.113), channel_id=1, source_target_pairs={{0,4},{2,6},{4,0},{6,2},{1,5},{3,7},{5,1},{7,3},{8,12},{10,14},{12... | collective-permute-start | bytes 786440 | tf_op jit(solution)/shard_map/ppermute | solution.py:559
  14.0 22.4 %collective-permute-start.6 = (bf16[128,1024]{1,0:T(8,128)(2,1)S(1)}, bf16[128,1024]{1,0:T(8,128)(2,1)}, u32[]{:S(2)}, u32[]{:S(2)}) collective-permute-start(bf16[128,1024]{1,0:T(8,128)(2,1)S(1)} %get-tuple-element.113), channel_id=1, source_target_pairs={{0,2},{2,4},{4,6},{6,0},{1,3},{3,5},{5,7},{7,1},{8,10},{10,12},{12... | collective-permute-start | bytes 786440 | tf_op jit(solution)/shard_map/ppermute | solution.py:559
  20.0 5.0 copy-start.11
  20.0 57.4 %collective-permute-start = (bf16[256,4096]{1,0:T(8,128)(2,1)}, bf16[256,4096]{1,0:T(8,128)(2,1)}, u32[]{:S(2)}, u32[]{:S(2)}) collective-permute-start(bf16[256,4096]{1,0:T(8,128)(2,1)} %pick_channels.4), channel_id=1, source_target_pairs={{0,1},{1,0},{2,3},{3,2},{4,5},{5,4},{6,7},{7,6},{8,9},{9,8},{10,11... | collective-permute-start | bytes 6291464 | tf_op jit(solution)/shard_map/ppermute | solution.py:599
  24.6 52.8 %collective-permute-start.9 = (bf16[256,4096]{1,0:T(8,128)(2,1)}, bf16[256,4096]{1,0:T(8,128)(2,1)S(1)}, u32[]{:S(2)}, u32[]{:S(2)}) collective-permute-start(bf16[256,4096]{1,0:T(8,128)(2,1)} %pick_channels.7), channel_id=1, source_target_pairs={{0,1},{1,0},{2,3},{3,2},{4,5},{5,4},{6,7},{7,6},{8,9},{9,8},{10,11... | collective-permute-start | bytes 6291464 | tf_op jit(solution)/shard_map/ppermute | solution.py:599
  38.7 36.2 %all-to-all-start = ((bf16[256,8,256]{0,2,1:T(8,128)(2,1)}), bf16[256,8,256]{0,2,1:T(8,128)(2,1)S(1)}, u32[]{:S(2)}, u32[]{:S(2)}) async-start(bf16[256,8,256]{0,2,1:T(8,128)(2,1)} %bitcast.21), calls=%async_computation | async-start | bytes 2097152 | tf_op jit(solution)/shard_map/all_to_all | solution.py:585
  42.8 286.9 %all-gather.3.cloned.1.call-start = ((), (), s32[]{:S(2)}) async-start(), calls=%async_computation.8 | async-start | bytes 4456448 | tf_op jit(solution)/shard_map/all_gather | solution.py:564
  74.9 1.0 copy-start.4
  77.4 135.5 %copy-start.3 = (bf16[8,256,256]{2,1,0:T(8,128)(2,1)}, bf16[8,256,256]{2,1,0:T(8,128)(2,1)S(1)}, u32[]{:S(2)}) copy-start(bf16[8,256,256]{2,1,0:T(8,128)(2,1)S(1)} %copy.40) | copy-start | bytes 3145732
  77.4 6.8 %copy-start.20 = (s32[8]{0:T(128)S(1)}, s32[8]{0:T(128)}, u32[]{:S(2)}) copy-start(s32[8]{0:T(128)} %param.27) | copy-start | bytes 100
  77.4 45.4 %copy-start.1 = (bf16[256,4096]{1,0:T(8,128)(2,1)}, bf16[256,4096]{1,0:T(8,128)(2,1)S(1)}, u32[]{:S(2)}) copy-start(bf16[256,4096]{1,0:T(8,128)(2,1)S(1)} %collective-permute-done.9.other_ref) | copy-start | bytes 6291460
  79.8 40.8 %all-to-all-start.1 = ((bf16[16,3,8192]{2,1,0:T(4,128)(2,1)}), bf16[16,3,8192]{2,1,0:T(4,128)(2,1)}, u32[]{:S(2)}, u32[]{:S(2)}) async-start(bf16[16,3,8192]{2,1,0:T(4,128)(2,1)} %broadcast_in_dim.137), calls=%async_computation.1 | async-start | bytes 2097152 | tf_op jit(solution)/shard_map/all_to_all | solution.py:644
  84.9 41.8 %copy-start.19 = (s32[16]{0:T(128)}, s32[16]{0:T(128)S(1)}, u32[]{:S(2)}) copy-start(s32[16]{0:T(128)S(1)} %get-tuple-element.111) | copy-start | bytes 196
  126.7 199.4 %all-to-all-start.2 = ((bf16[256,8,512]{2,0,1:T(8,128)(2,1)}), bf16[256,8,512]{2,0,1:T(8,128)(2,1)}, u32[]{:S(2)}, u32[]{:S(2)}) async-start(bf16[256,8,512]{2,0,1:T(8,128)(2,1)} %bitcast.46), calls=%async_computation.2 | async-start | bytes 4194304 | tf_op jit(solution)/shard_map/all_to_all | solution.py:693
  135.5 5.0 copy-start.16
  135.5 5.0 copy-start.18
  135.6 14.9 %copy-start.5 = (bf16[256,512]{1,0:T(8,128)(2,1)S(1)}, bf16[256,512]{1,0:T(8,128)(2,1)}, u32[]{:S(2)}) copy-start(bf16[256,512]{1,0:T(8,128)(2,1)} %low_own_ref.3) | copy-start | bytes 786436
  135.6 76.1 %collective-permute-start.1 = (bf16[256,4096]{1,0:T(8,128)(2,1)}, bf16[256,4096]{1,0:T(8,128)(2,1)}, u32[]{:S(2)}, u32[]{:S(2)}) collective-permute-start(bf16[256,4096]{1,0:T(8,128)(2,1)} %pick_channels.5), channel_id=1, source_target_pairs={{0,1},{1,0},{2,3},{3,2},{4,5},{5,4},{6,7},{7,6},{8,9},{9,8},{10,11... | collective-permute-start | bytes 6291464 | tf_op jit(solution)/shard_map/ppermute | solution.py:637
  140.5 72.4 %collective-permute-start.2 = (bf16[256,4096]{1,0:T(8,128)(2,1)}, bf16[256,4096]{1,0:T(8,128)(2,1)S(1)}, u32[]{:S(2)}, u32[]{:S(2)}) collective-permute-start(bf16[256,4096]{1,0:T(8,128)(2,1)} %pick_channels.6), channel_id=1, source_target_pairs={{0,1},{1,0},{2,3},{3,2},{4,5},{5,4},{6,7},{7,6},{8,9},{9,8},{10,11... | collective-permute-start | bytes 6291464 | tf_op jit(solution)/shard_map/ppermute | solution.py:637
  142.7 35.3 %collective-permute-start.5 = (f32[24,2048]{1,0:T(8,128)}, f32[24,2048]{1,0:T(8,128)}, u32[]{:S(2)}, u32[]{:S(2)}) collective-permute-start(f32[24,2048]{1,0:T(8,128)} %concatenate.24), channel_id=1, source_target_pairs={{0,6},{2,0},{4,2},{6,4},{1,7},{3,1},{5,3},{7,5},{8,14},{10,8},{12,... | collective-permute-start | bytes 589832 | tf_op jit(solution)/shard_map/ppermute | solution.py:641
  146.4 4.8 collective-permute-start.11
  149.3 60.9 %collective-permute-start.12 = (bf16[4,128,1024]{2,1,0:T(8,128)(2,1)}, bf16[4,128,1024]{2,1,0:T(8,128)(2,1)}, u32[]{:S(2)}, u32[]{:S(2)}) collective-permute-start(bf16[4,128,1024]{2,1,0:T(8,128)(2,1)} %pad_maximum_fusion.1.refs_0_), channel_id=1, source_target_pairs={{0,8},{8,0},{16,24},{24,16},{1,9},{9,1},{17,25},{25,17},{2,10},{10... | collective-permute-start | bytes 3145736 | tf_op jit(solution)/shard_map/ppermute | solution.py:562
  151.2 48.0 %collective-permute-start.4 = (f32[24,2048]{1,0:T(8,128)}, f32[24,2048]{1,0:T(8,128)}, u32[]{:S(2)}, u32[]{:S(2)}) collective-permute-start(f32[24,2048]{1,0:T(8,128)} %concatenate.24), channel_id=1, source_target_pairs={{0,4},{2,6},{4,0},{6,2},{1,5},{3,7},{5,1},{7,3},{8,12},{10,14},{12... | collective-permute-start | bytes 589832 | tf_op jit(solution)/shard_map/ppermute | solution.py:641
  178.0 31.4 %collective-permute-start.10 = (bf16[256,512]{1,0:T(8,128)(2,1)S(1)}, bf16[256,512]{1,0:T(8,128)(2,1)}, u32[]{:S(2)}, u32[]{:S(2)}) collective-permute-start(bf16[256,512]{1,0:T(8,128)(2,1)S(1)} %copy-done.5), channel_id=1, source_target_pairs={{0,1},{1,0},{2,3},{3,2},{4,5},{5,4},{6,7},{7,6},{8,9},{9,8},{10,11... | collective-permute-start | bytes 786440 | tf_op jit(solution)/shard_map/ppermute | solution.py:602
  199.2 8.9 %collective-permute-start.3 = (f32[24,2048]{1,0:T(8,128)}, f32[24,2048]{1,0:T(8,128)S(1)}, u32[]{:S(2)}, u32[]{:S(2)}) collective-permute-start(f32[24,2048]{1,0:T(8,128)} %concatenate.24), channel_id=1, source_target_pairs={{0,2},{2,4},{4,6},{6,0},{1,3},{3,5},{5,7},{7,1},{8,10},{10,12},{12... | collective-permute-start | bytes 589832 | tf_op jit(solution)/shard_map/ppermute | solution.py:641
  208.1 6.3 %copy-start.14 = (f32[24,2048]{1,0:T(8,128)}, f32[24,2048]{1,0:T(8,128)S(1)}, u32[]{:S(2)}) copy-start(f32[24,2048]{1,0:T(8,128)S(1)} %collective-permute-done.3) | copy-start | bytes 589828
  208.1 51.0 %collective-permute-start.13 = (bf16[4,128,1024]{2,1,0:T(8,128)(2,1)}, bf16[4,128,1024]{2,1,0:T(8,128)(2,1)}, u32[]{:S(2)}, u32[]{:S(2)}) collective-permute-start(bf16[4,128,1024]{2,1,0:T(8,128)(2,1)} %pad_maximum_fusion.1.refs_0_), channel_id=1, source_target_pairs={{0,16},{8,24},{16,0},{24,8},{1,17},{9,25},{17,1},{25,9},{2,18},{10... | collective-permute-start | bytes 3145736 | tf_op jit(solution)/shard_map/ppermute | solution.py:562
  209.3 49.8 %collective-permute-start.14 = (bf16[4,128,1024]{2,1,0:T(8,128)(2,1)}, bf16[4,128,1024]{2,1,0:T(8,128)(2,1)}, u32[]{:S(2)}, u32[]{:S(2)}) collective-permute-start(bf16[4,128,1024]{2,1,0:T(8,128)(2,1)} %pad_maximum_fusion.1.refs_0_), channel_id=1, source_target_pairs={{0,24},{8,16},{16,8},{24,0},{1,25},{9,17},{17,9},{25,1},{2,26},{10... | collective-permute-start | bytes 3145736 | tf_op jit(solution)/shard_map/ppermute | solution.py:562
  210.2 115.9 %collective-permute-start.15 = (bf16[2048,256]{1,0:T(8,128)(2,1)S(1)}, bf16[2048,256]{1,0:T(8,128)(2,1)}, u32[]{:S(2)}, u32[]{:S(2)}) collective-permute-start(bf16[2048,256]{1,0:T(8,128)(2,1)S(1)} %bitcast.52), channel_id=1, source_target_pairs={{0,8},{8,0},{16,24},{24,16},{1,9},{9,1},{17,25},{25,17},{2,10},{10... | collective-permute-start | bytes 3145736 | tf_op jit(solution)/shard_map/ppermute | solution.py:694
  211.6 114.5 %collective-permute-start.16 = (bf16[2048,256]{1,0:T(8,128)(2,1)S(1)}, bf16[2048,256]{1,0:T(8,128)(2,1)}, u32[]{:S(2)}, u32[]{:S(2)}) collective-permute-start(bf16[2048,256]{1,0:T(8,128)(2,1)S(1)} %bitcast.53), channel_id=1, source_target_pairs={{0,16},{8,24},{16,0},{24,8},{1,17},{9,25},{17,1},{25,9},{2,18},{10... | collective-permute-start | bytes 3145736 | tf_op jit(solution)/shard_map/ppermute | solution.py:694
  212.8 8.7 %copy-start.2 = (bf16[256,4096]{1,0:T(8,128)(2,1)}, bf16[256,4096]{1,0:T(8,128)(2,1)S(1)}, u32[]{:S(2)}) copy-start(bf16[256,4096]{1,0:T(8,128)(2,1)S(1)} %collective-permute-done.2.refs_7_) | copy-start | bytes 6291460
  212.8 113.3 %collective-permute-start.17 = (bf16[2048,256]{1,0:T(8,128)(2,1)S(1)}, bf16[2048,256]{1,0:T(8,128)(2,1)}, u32[]{:S(2)}, u32[]{:S(2)}) collective-permute-start(bf16[2048,256]{1,0:T(8,128)(2,1)S(1)} %bitcast.54), channel_id=1, source_target_pairs={{0,24},{8,16},{16,8},{24,0},{1,25},{9,17},{17,9},{25,1},{2,26},{10... | collective-permute-start | bytes 3145736 | tf_op jit(solution)/shard_map/ppermute | solution.py:694
  217.6 3.0 copy-start.12
  217.6 3.0 copy-start.13
  217.6 41.5 %copy-start.15 = (f32[8192]{0:T(1024)S(1)}, f32[8192]{0:T(1024)}, u32[]{:S(2)}) copy-start(f32[8192]{0:T(1024)} %reshape.113) | copy-start | bytes 98308
  218.9 42.8 %copy-start = (f32[4,24,2048]{2,1,0:T(8,128)}, f32[4,24,2048]{2,1,0:T(8,128)S(1)}, u32[]{:S(2)}) copy-start(f32[4,24,2048]{2,1,0:T(8,128)S(1)} %pad_maximum_fusion.2.param_ref.refs_3_.refs_4_) | copy-start | bytes 2359300
  326.1 38.4 %all-to-all-start.3 = ((bf16[16,32,256]{2,1,0:T(8,128)(2,1)}), bf16[16,32,256]{2,1,0:T(8,128)(2,1)S(1)}, u32[]{:S(2)}, u32[]{:S(2)}) async-start(bf16[16,32,256]{2,1,0:T(8,128)(2,1)} %get-tuple-element.69), calls=%async_computation.3 | async-start | bytes 524288 | tf_op jit(solution)/shard_map/all_to_all | solution.py:676
  364.5 0.7 copy-start.9
  367.7 43.5 %all-to-all-start.4 = ((bf16[16,16,256]{2,1,0:T(8,128)(2,1)}), bf16[16,16,256]{2,1,0:T(8,128)(2,1)S(1)}, u32[]{:S(2)}, u32[]{:S(2)}) async-start(bf16[16,16,256]{2,1,0:T(8,128)(2,1)} %state_combine.2), calls=%async_computation.4 | async-start | bytes 262144 | tf_op jit(solution)/shard_map/all_to_all | solution.py:676
  374.6 34.9 %copy-start.17 = (bf16[8,32,256]{2,1,0:T(8,128)(2,1)S(1)}, bf16[8,32,256]{2,1,0:T(8,128)(2,1)}, u32[]{:S(2)}) copy-start(bf16[8,32,256]{2,1,0:T(8,128)(2,1)} %get-tuple-element.74) | copy-start | bytes 393220
  411.2 65.1 %copy-start.10 = (bf16[16,16,256]{2,1,0:T(8,128)(2,1)}, bf16[16,16,256]{2,1,0:T(8,128)(2,1)S(1)}, u32[]{:S(2)}) copy-start(bf16[16,16,256]{2,1,0:T(8,128)(2,1)S(1)} %all-to-all-done.4.refs_2_) | copy-start | bytes 393220
  411.2 65.1 %all-to-all-start.5 = ((bf16[16,32,256]{2,1,0:T(8,128)(2,1)}), bf16[16,32,256]{2,1,0:T(8,128)(2,1)S(1)}, u32[]{:S(2)}, u32[]{:S(2)}) async-start(bf16[16,32,256]{2,1,0:T(8,128)(2,1)} %pad_maximum_fusion.5), calls=%async_computation.5 | async-start | bytes 524288 | tf_op jit(solution)/shard_map/all_to_all | solution.py:676
  476.3 0.7 copy-start.8
  479.6 49.3 %all-to-all-start.6 = ((bf16[16,16,256]{2,1,0:T(8,128)(2,1)}), bf16[16,16,256]{2,1,0:T(8,128)(2,1)S(1)}, u32[]{:S(2)}, u32[]{:S(2)}) async-start(bf16[16,16,256]{2,1,0:T(8,128)(2,1)} %state_combine.3), calls=%async_computation.6 | async-start | bytes 262144 | tf_op jit(solution)/shard_map/all_to_all | solution.py:676
  528.9 0.7 copy-start.6
  529.6 64.2 %all-to-all-start.7 = ((bf16[8,256,512]{2,1,0:T(8,128)(2,1)}), bf16[8,256,512]{2,1,0:T(8,128)(2,1)S(1)}, u32[]{:S(2)}, u32[]{:S(2)}) async-start(bf16[8,256,512]{2,1,0:T(8,128)(2,1)} %bitcast.31), calls=%async_computation.7 | async-start | bytes 4194304 | tf_op jit(solution)/shard_map/all_to_all | solution.py:713
  534.6 48.4 %collective-permute-start.18 = (bf16[256,4096]{1,0:T(8,128)(2,1)}, bf16[256,4096]{1,0:T(8,128)(2,1)}, u32[]{:S(2)}, u32[]{:S(2)}) collective-permute-start(bf16[256,4096]{1,0:T(8,128)(2,1)} %get-tuple-element.106), channel_id=1, source_target_pairs={{0,1},{1,0},{2,3},{3,2},{4,5},{5,4},{6,7},{7,6},{8,9},{9,8},{10,11... | collective-permute-start | bytes 6291464 | tf_op jit(solution)/shard_map/ppermute | solution.py:712
  558.7 28.7 %collective-permute-start.19 = (bf16[256,2048]{1,0:T(8,128)(2,1)}, bf16[256,2048]{1,0:T(8,128)(2,1)S(1)}, u32[]{:S(2)}, u32[]{:S(2)}) collective-permute-start(bf16[256,2048]{1,0:T(8,128)(2,1)} %get-tuple-element.107), channel_id=1, source_target_pairs={{0,1},{1,0},{2,3},{3,2},{4,5},{5,4},{6,7},{7,6},{8,9},{9,8},{10,11... | collective-permute-start | bytes 3145736 | tf_op jit(solution)/shard_map/ppermute | solution.py:715
  582.3 8.7 %collective-permute-start.20 = (bf16[256,2048]{1,0:T(8,128)(2,1)}, bf16[256,2048]{1,0:T(8,128)(2,1)}, u32[]{:S(2)}, u32[]{:S(2)}) collective-permute-start(bf16[256,2048]{1,0:T(8,128)(2,1)} %get-tuple-element.108), channel_id=1, source_target_pairs={{0,1},{1,0},{2,3},{3,2},{4,5},{5,4},{6,7},{7,6},{8,9},{9,8},{10,11... | collective-permute-start | bytes 3145736 | tf_op jit(solution)/shard_map/ppermute | solution.py:717
  587.4 1.0 copy-start.7
Sparse Core Ops, SparseCore 0:
  46.3 102.5 all-gather.2
where the time goes:
time: 604 us; the launch traced here: 602 us
  Pallas kernels  315 us (52%)
  waiting for transfers between devices  165 us (27%)
  starting transfers between devices  59.5 us (10%)
  local copies, waits for them, and re-layouts  28.1 us (5%)
  other arithmetic  17 us (3%)
  between operations  15.7 us (3%)
    pallas_call x3, Pallas kernels, run_scan(): pl.pallas_call(functools.partial(scan_kernel, sources=sources), grid_spec...  134 us
    pallas_call x3, Pallas kernels, run_correct(): pl.pallas_call(functools.partial(correct_kernel, resumed=resumed), grid_s...  89.7 us
    pallas_call x1, Pallas kernels, run_flash(): pl.pallas_call(functools.partial(flash_kernel, heads=heads, rows=rows, so...  58.2 us
    ppermute x3, waiting for transfers between devices, local(): lax.ppermute(packed, 'chip', move)  52.4 us
    ppermute x3, waiting for transfers between devices, local(): lax.ppermute(shards_first, 'blk', move)  37.6 us
    all_to_all x1, waiting for transfers between devices, local(): lax.all_to_all(jnp.broadcast_to(tail[None], (chunks, CONV - 1, PIECES * c...  35 us
    all_to_all x1, waiting for transfers between devices, local(): lax.all_to_all(kv_rows, ulys, split_axis=1, concat_axis=0, tiled=True)  30.1 us
    all_to_all x4, starting transfers between devices, to_owners(): return lax.all_to_all(array, chips, split_axis=0, concat_axis=0, tiled=True)  24.2 us
  transfers between devices with their start and end apart: 30, of which 7 were waited for; matrix products, arithmetic and copies ran while one was open for 7% of the time, Pallas kernels for 51%

commit v1 on v0

--- a/solution.py
+++ b/solution.py
@@ -558,9 +558,6 @@
     shards_first = jnp.stack(
         [part_first] + [lax.ppermute(part_first, "chip", move) for move in far_moves]
     )
-    weights_first = [shards_first] + [
-        lax.ppermute(shards_first, "blk", move) for move in flips
-    ]
     weights_later = lax.all_gather(part_later, chips, axis=0, tiled=False)
     weights_later = [weights_later.reshape(blk_count, chip_count, part_rows, width)]
 
@@ -573,6 +570,41 @@
             axis=1,
         )
 
+    per_block = SPAN // tokens
+    chunk_ids = jnp.arange(chunks, dtype=jnp.int32)
+    stored = chunk_ids // per_block
+    block_ids = jnp.arange(block_total, dtype=jnp.int32)
+    block_pos = jnp.sum(
+        jnp.where(stored[:, None] == block_ids[None, :], span_order[None, :], 0), axis=1
+    )
+    chunk_pos = block_pos * per_block + chunk_ids % per_block
+    order = jnp.sum(
+        jnp.where(chunk_pos[None, :] == chunk_ids[:, None], chunk_ids[None, :], 0), axis=1
+    ).astype(jnp.int32)
+    me = blk * chip_count + chip
+    my_pos = jnp.sum(jnp.where(chunk_ids == me, chunk_pos, 0))
+    last_rows = mamba_input[half - (CONV - 1) :].reshape(
+        CONV - 1, chip_count, PAIR, PIECES, width
+    )
+
+    def columns_of(side):
+        mine = lax.dynamic_index_in_dim(last_rows, side, 2, False)
+        return mine.swapaxes(1, 2).reshape(CONV - 1, PIECES * cols)
+
+    tail = jnp.where(
+        core == 1, columns_of(core), lax.ppermute(columns_of(1 - core), "core", swap)
+    )
+    tails = lax.all_to_all(
+        jnp.broadcast_to(tail[None], (chunks, CONV - 1, PIECES * cols)), chips,
+        split_axis=0, concat_axis=0, tiled=True,
+    )
+    before = (chunk_pos == my_pos - 1).astype(jnp.bfloat16)
+    halo = jnp.einsum("m,mkc->kc", before, tails, preferred_element_type=jnp.float32)
+    halo = jnp.concatenate(
+        [jnp.zeros((8 - (CONV - 1), PIECES * cols), jnp.bfloat16), halo.astype(jnp.bfloat16)],
+        axis=0,
+    )
+
     kv_heads = key_rows.shape[1] // HD
     repeat = ulys_count // kv_heads
     kv_rows = jnp.stack(
@@ -581,7 +613,10 @@
     kv_rows = jnp.broadcast_to(
         kv_rows[:, :, None], (half, kv_heads, repeat, 2, HD)
     ).reshape(half, ulys_count * 2 * HD)
-    kv_rows, _ = lax.optimization_barrier((kv_rows, shards_first))
+    kv_rows, shards_first, halo = lax.optimization_barrier((kv_rows, shards_first, halo))
+    weights_first = [shards_first] + [
+        lax.ppermute(shards_first, "blk", move) for move in flips
+    ]
     kv_local = lax.all_to_all(kv_rows, ulys, split_axis=1, concat_axis=0, tiled=True)
 
     packed = jnp.concatenate(
@@ -614,43 +649,12 @@
         same[:, :, None], mixers[:, None, STATE:], jnp.zeros((), jnp.bfloat16)
     ).reshape(tokens, GROUP * STATE)
 
-    per_block = SPAN // tokens
-    chunk_ids = jnp.arange(chunks, dtype=jnp.int32)
-    stored = chunk_ids // per_block
-    block_ids = jnp.arange(block_total, dtype=jnp.int32)
-    block_pos = jnp.sum(
-        jnp.where(stored[:, None] == block_ids[None, :], span_order[None, :], 0), axis=1
-    )
-    chunk_pos = block_pos * per_block + chunk_ids % per_block
-    order = jnp.sum(
-        jnp.where(chunk_pos[None, :] == chunk_ids[:, None], chunk_ids[None, :], 0), axis=1
-    ).astype(jnp.int32)
-    me = blk * chip_count + chip
-    my_pos = jnp.sum(jnp.where(chunk_ids == me, chunk_pos, 0))
-    own_tail = lax.dynamic_index_in_dim(
-        mamba_input[half - (CONV - 1) :].reshape(CONV - 1, chip_count, PAIR, PIECES, width),
-        core, 2, False,
-    ).swapaxes(1, 2).reshape(CONV - 1, PIECES * cols)
-    other_tail = jnp.concatenate([x[half - (CONV - 1) :] for x in x_other], axis=1)
-    tail = jnp.where(core == 1, own_tail, other_tail)
     gate_other = [
         lax.ppermute(run_pick(core_arr, gate_input, piece, width), "core", swap)
         for piece in range(PIECES)
     ]
 
     params = jnp.stack([packed] + [lax.ppermute(packed, "chip", move) for move in far_moves])
-
-    kv_local, tail = lax.optimization_barrier((kv_local, tail))
-    tails = lax.all_to_all(
-        jnp.broadcast_to(tail[None], (chunks, CONV - 1, PIECES * cols)), chips,
-        split_axis=0, concat_axis=0, tiled=True,
-    )
-    before = (chunk_pos == my_pos - 1).astype(jnp.bfloat16)
-    halo = jnp.einsum("m,mkc->kc", before, tails, preferred_element_type=jnp.float32)
-    halo = jnp.concatenate(
-        [jnp.zeros((8 - (CONV - 1), PIECES * cols), jnp.bfloat16), halo.astype(jnp.bfloat16)],
-        axis=0,
-    )
 
     share = cols // chunks
     split = chip_count // 2
@@ -685,13 +689,18 @@
     lows_first = (by_flip(delta_low), by_flip(low_other))
     lows_later = (delta_low, low_other)
     tables = flash_tables(span_order, my_blocks, blk)
-    x_now, gate_other, my_rates, tables, order = lax.optimization_barrier(
-        (x_other[0], gate_other, my_rates, tables, order)
-    )
-    made_0 = scan_part(0, x_now, lows_first, weights_first, 0, chip_count)
-    halo, queries, kv_local = lax.optimization_barrier((halo, queries, kv_local))
+    (
+        queries, kv_local, gate_other, inject, read, params, my_rates, tables, order, lows_first,
+        x_other,
+    ) = lax.optimization_barrier(
+        (
+            queries, kv_local, gate_other, inject, read, params, my_rates, tables, order,
+            lows_first, x_other,
+        )
+    )
     q_local = lax.all_to_all(queries, ulys, split_axis=1, concat_axis=0, tiled=True)
     kv_parts = [kv_local] + [lax.ppermute(kv_local, "blk", move) for move in flips]
+    made_0 = scan_part(0, x_other[0], lows_first, weights_first, 0, chip_count)
     x_now, sent_0, q_local, kv_parts, my_rates = lax.optimization_barrier(
         (x_other[1], made_0[2], q_local, kv_parts, my_rates)
     )

time: 604 us -> 561 us (0.929)
  waiting for transfers between devices: 165 us -> 107 us
  starting transfers between devices: 59.5 us -> 75.7 us
    all_to_all x1, waiting for transfers between devices: 30.1 us -> 0.01 us  [local(): lax.all_to_all(kv_rows, ulys, split_axis=1, concat_axis=0, tiled=True)]
    all_to_all x1, waiting for transfers between devices: 35 us -> 19.5 us  [local(): lax.all_to_all(jnp.broadcast_to(tail[None], (chunks, CONV - 1, PIECES * c...]
    ppermute x3, waiting for transfers between devices: 8.9 us -> 0.01 us  [local(): lax.ppermute(part_first, 'chip', move)]
    ppermute x3, starting transfers between devices: 3.73 us -> 12.6 us  [local(): lax.ppermute(packed, 'chip', move)]
  transfers between devices with their start and end apart: 30 -> 31, of which waited for: 7 -> 6; matrix products, arithmetic and copies ran while one was open for 7% -> 7% of each run, Pallas kernels for 51% -> 55%
where the time goes in v1:
time: 561 us; the launch traced here: 559 us
  Pallas kernels  315 us (56%)
  waiting for transfers between devices  107 us (19%)
  starting transfers between devices  75.7 us (13%)
  local copies, waits for them, and re-layouts  25.9 us (5%)
  other arithmetic  17.8 us (3%)
  between operations  15.9 us (3%)
    pallas_call x3, Pallas kernels, run_scan(): pl.pallas_call(functools.partial(scan_kernel, sources=sources), grid_spec...  134 us
    pallas_call x3, Pallas kernels, run_correct(): pl.pallas_call(functools.partial(correct_kernel, resumed=resumed), grid_s...  89.7 us
    pallas_call x1, Pallas kernels, run_flash(): pl.pallas_call(functools.partial(flash_kernel, heads=heads, rows=rows, so...  58.3 us
    ppermute x3, waiting for transfers between devices, local(): lax.ppermute(packed, 'chip', move)  48 us
    ppermute x3, waiting for transfers between devices, local(): lax.ppermute(shards_first, 'blk', move)  39.3 us
    all_to_all x4, starting transfers between devices, to_owners(): return lax.all_to_all(array, chips, split_axis=0, concat_axis=0, tiled=True)  26.7 us
    all_to_all x1, waiting for transfers between devices, local(): lax.all_to_all(jnp.broadcast_to(tail[None], (chunks, CONV - 1, PIECES * c...  19.5 us
    pallas_call x4, Pallas kernels, run_pick(): pl.pallas_call(copy_kernel, grid_spec=pltpu.PrefetchScalarGridSpec(num_sc...  18 us
  transfers between devices with their start and end apart: 31, of which 6 were waited for; matrix products, arithmetic and copies ran while one was open for 7% of the time, Pallas kernels for 55%

profile of v1, /device:TPU:0, one launch (start us, length us, event | category | flops | bytes accessed | tf_op | source)
XLA Modules:
  0.0 558.8 jit_solution(6787699811880169323)
XLA Ops:
  7.2 1.9 fusion.12
  9.1 5.1 collective-permute-start.2
  14.2 1.0 collective-permute-start
  15.2 1.0 slice.23
  17.2 4.5 pick_channels.4
  22.2 4.6 pick_channels.5
  27.1 1.4 broadcast_in_dim.125
  28.5 6.1 %all-to-all-start = ((bf16[16,3,8192]{2,1,0:T(4,128)(2,1)}), bf16[16,3,8192]{2,1,0:T(4,128)(2,1)S(1)}, u32[]{:S(2)}, u32[]{:S(2)}) async-start(bf16[16,3,8192]{2,1,0:T(4,128)(2,1)} %broadcast_in_dim.125), calls=%async_computation | async-start | bytes 2097152 | tf_op jit(solution)/shard_map/all_to_all | solution.py:597
  36.1 0.7 fusion.8
  38.5 4.5 pick_channels.6
  43.0 4.5 pick_channels.7
  47.5 2.1 copy.39
  49.6 2.0 copy.38
  52.3 0.7 constant_dynamic-slice_fusion.7
  53.0 2.3 pad_maximum_fusion
  56.0 2.3 pad_maximum_fusion.1.refs_0_
  58.4 19.5 %all-to-all-done = bf16[16,3,8192]{2,1,0:T(4,128)(2,1)S(1)} async-done(((bf16[16,3,8192]{2,1,0:T(4,128)(2,1)}), bf16[16,3,8192]{2,1,0:T(4,128)(2,1)S(1)}, u32[]{:S(2)}, u32[]{:S(2)}) %all-to-all-start) | async-done | bytes 786464 | tf_op jit(solution)/shard_map/all_to_all | solution.py:597
  77.9 1.6 fusion
  80.3 4.3 all-to-all-start.1
  85.1 1.9 compare_convert_fusion
  87.2 3.8 collective-permute-start.9
  91.5 0.8 maximum_select_fusion
  92.3 32.6 %collective-permute-done.9 = f32[24,2048]{1,0:T(8,128)S(1)} collective-permute-done((f32[24,2048]{1,0:T(8,128)S(1)}, f32[24,2048]{1,0:T(8,128)S(1)}, u32[]{:S(2)}, u32[]{:S(2)}) %collective-permute-start.9) | collective-permute-done | bytes 196640 | tf_op jit(solution)/shard_map/ppermute | solution.py:657
  124.9 8.2 %collective-permute-start.8 = (f32[24,2048]{1,0:T(8,128)S(1)}, f32[24,2048]{1,0:T(8,128)S(1)}, u32[]{:S(2)}, u32[]{:S(2)}) collective-permute-start(f32[24,2048]{1,0:T(8,128)S(1)} %concatenate.24), channel_id=1, source_target_pairs={{0,4},{2,6},{4,0},{6,2},{1,5},{3,7},{5,1},{7,3},{8,12},{10,14},{12... | collective-permute-start | bytes 589832 | tf_op jit(solution)/shard_map/ppermute | solution.py:657
  133.3 0.7 reshape.117
  134.0 8.4 %collective-permute-done.8 = f32[24,2048]{1,0:T(8,128)S(1)} collective-permute-done((f32[24,2048]{1,0:T(8,128)S(1)}, f32[24,2048]{1,0:T(8,128)S(1)}, u32[]{:S(2)}, u32[]{:S(2)}) %collective-permute-start.8) | collective-permute-done | bytes 196640 | tf_op jit(solution)/shard_map/ppermute | solution.py:657
  143.0 0.8 broadcast_select_fusion
  143.8 7.0 %collective-permute-done.7 = f32[24,2048]{1,0:T(8,128)S(1)} collective-permute-done((f32[24,2048]{1,0:T(8,128)S(1)}, f32[24,2048]{1,0:T(8,128)S(1)}, u32[]{:S(2)}, u32[]{:S(2)}) %collective-permute-start.7) | collective-permute-done | bytes 196640 | tf_op jit(solution)/shard_map/ppermute | solution.py:657
  150.8 1.2 pad_maximum_fusion.2.param_ref.refs_3_.refs_4_
  151.9 0.7 multiply_bitcast_fusion
  152.7 1.8 pad_maximum_fusion.3
  154.5 2.3 copy.42
  156.8 3.5 broadcast_in_dim.128.inject_ref
  160.4 1.5 copy.62
  161.9 3.7 all-to-all-start.2
  165.7 1.6 collective-permute-start.13
  167.3 1.5 collective-permute-start.14
  169.2 1.5 collective-permute-start.16
  170.7 1.5 collective-permute-start.17
  172.2 19.5 %collective-permute-done.13.refs_1_ = bf16[4,128,1024]{2,1,0:T(8,128)(2,1)S(1)} collective-permute-done((bf16[4,128,1024]{2,1,0:T(8,128)(2,1)S(1)}, bf16[4,128,1024]{2,1,0:T(8,128)(2,1)S(1)}, u32[]{:S(2)}, u32[]{:S(2)}) %collective-permute-start.13) | collective-permute-done | bytes 1048608 | tf_op jit(solution)/shard_map/ppermute | solution.py:618
  191.8 1.0 copy-done.8
  192.8 2.4 collective-permute-start.18
  195.2 0.9 copy.44.read_ref.refs_4_.refs_5_
  196.1 19.8 %collective-permute-done.14.refs_2_ = bf16[4,128,1024]{2,1,0:T(8,128)(2,1)} collective-permute-done((bf16[4,128,1024]{2,1,0:T(8,128)(2,1)S(1)}, bf16[4,128,1024]{2,1,0:T(8,128)(2,1)}, u32[]{:S(2)}, u32[]{:S(2)}) %collective-permute-start.14) | collective-permute-done | bytes 1048608 | tf_op jit(solution)/shard_map/ppermute | solution.py:618
  215.9 64.3 %token_scan.3 = (f32[32,512,128]{2,1,0:T(8,128)}, bf16[512,4096]{1,0:T(8,128)(2,1)}, bf16[16,32,256]{2,1,0:T(8,128)(2,1)}) custom-call(s32[2]{0:T(128)} %pad_add_fusion.core_ref, bf16[256,16384]{1,0:T(8,128)(2,1)} %own_ref.5, bf16[256,4096]{1,0:T(8,128)(2,1)} %collective-permute-done.11.other_ref, bf16[8,8192]{1,0:T(8,128)(2,1)} %concatenate.21.halo_ref, ...), custom_call_target="tpu_custom_call" | custom-call | tf_op jit(solution)/shard_map/token_scan/pallas_call | solution.py:370
  280.3 6.0 %all-to-all-start.3 = ((bf16[16,32,256]{2,1,0:T(8,128)(2,1)}), bf16[16,32,256]{2,1,0:T(8,128)(2,1)S(1)}, u32[]{:S(2)}, u32[]{:S(2)}) async-start(bf16[16,32,256]{2,1,0:T(8,128)(2,1)} %get-tuple-element.80), calls=%async_computation.3 | async-start | bytes 524288 | tf_op jit(solution)/shard_map/all_to_all | solution.py:680
  286.3 34.8 %token_scan.4 = (f32[16,512,128]{2,1,0:T(8,128)}, bf16[512,2048]{1,0:T(8,128)(2,1)}, bf16[8,32,256]{2,1,0:T(8,128)(2,1)}) custom-call(s32[2]{0:T(128)} %pad_add_fusion.core_ref, bf16[256,16384]{1,0:T(8,128)(2,1)} %own_ref.5, bf16[256,4096]{1,0:T(8,128)(2,1)} %collective-permute-done.12.other_ref, bf16[8,8192]{1,0:T(8,128)(2,1)} %concatenate.21.halo_ref, ...), custom_call_target="tpu_custom_call" | custom-call | tf_op jit(solution)/shard_map/token_scan/pallas_call | solution.py:370
  321.8 2.5 state_combine.2
  324.3 6.9 %all-to-all-start.4 = ((bf16[16,16,256]{2,1,0:T(8,128)(2,1)}), bf16[16,16,256]{2,1,0:T(8,128)(2,1)S(1)}, u32[]{:S(2)}, u32[]{:S(2)}) async-start(bf16[16,16,256]{2,1,0:T(8,128)(2,1)} %state_combine.2), calls=%async_computation.4 | async-start | bytes 262144 | tf_op jit(solution)/shard_map/all_to_all | solution.py:680
  331.2 35.0 %token_scan.5 = (f32[16,512,128]{2,1,0:T(8,128)}, bf16[512,2048]{1,0:T(8,128)(2,1)}, bf16[8,32,256]{2,1,0:T(8,128)(2,1)}) custom-call(s32[2]{0:T(128)} %pad_add_fusion.core_ref, bf16[256,16384]{1,0:T(8,128)(2,1)} %own_ref.5, bf16[256,4096]{1,0:T(8,128)(2,1)} %collective-permute-done.12.other_ref, bf16[8,8192]{1,0:T(8,128)(2,1)} %concatenate.21.halo_ref, ...), custom_call_target="tpu_custom_call" | custom-call | tf_op jit(solution)/shard_map/token_scan/pallas_call | solution.py:370
  366.2 1.6 pad_maximum_fusion.5
  367.8 6.9 %all-to-all-start.5 = ((bf16[16,32,256]{2,1,0:T(8,128)(2,1)}), bf16[16,32,256]{2,1,0:T(8,128)(2,1)S(1)}, u32[]{:S(2)}, u32[]{:S(2)}) async-start(bf16[16,32,256]{2,1,0:T(8,128)(2,1)} %pad_maximum_fusion.5), calls=%async_computation.5 | async-start | bytes 524288 | tf_op jit(solution)/shard_map/all_to_all | solution.py:680
  374.7 58.3 %causal_attention.1 = bf16[2048,512]{1,0:T(8,128)(2,1)} custom-call(s32[9]{0:T(128)} %compare_convert_fusion.2.side_ref, s32[9]{0:T(128)} %get-tuple-element.91.flip_ref, s32[9]{0:T(128)} %get-tuple-element.92.half_ref, s32[9]{0:T(128)} %get-tuple-element.95.diag_ref.last_ref, s32[9]{0:T(128)} %get-tuple-element.94.first_ref, ...), custom_call_target="tpu_custom_call" | custom-call | tf_op jit(solution)/shard_map/causal_attention/pallas_call | solution.py:489
  433.7 2.5 state_combine.3
  436.2 6.9 %all-to-all-start.6 = ((bf16[16,16,256]{2,1,0:T(8,128)(2,1)}), bf16[16,16,256]{2,1,0:T(8,128)(2,1)S(1)}, u32[]{:S(2)}, u32[]{:S(2)}) async-start(bf16[16,16,256]{2,1,0:T(8,128)(2,1)} %state_combine.3), calls=%async_computation.6 | async-start | bytes 262144 | tf_op jit(solution)/shard_map/all_to_all | solution.py:680
  443.2 42.4 %state_correction.3 = (bf16[256,16384]{1,0:T(8,128)(2,1)}, bf16[256,4096]{1,0:T(8,128)(2,1)}) custom-call(s32[2]{0:T(128)} %pad_add_fusion.core_ref, f32[32,512,128]{2,1,0:T(8,128)} %get-tuple-element.70.refs_0_, bf16[512,4096]{1,0:T(8,128)(2,1)} %get-tuple-element.71.refs_1_, bf16[16,16,256]{2,1,0:T(8,128)(2,1)} %copy-done.14, f32[4,24,2048]{2,1,0:T(8,128)} %copy-done, ...), custom_call_target="tpu_custom_call" | custom-call | tf_op jit(solution)/shard_map/state_correction/pallas_call | solution.py:422
  486.2 5.0 all-to-all-start.7
  491.7 23.6 %state_correction.4 = (bf16[256,16384]{1,0:T(8,128)(2,1)}, bf16[256,2048]{1,0:T(8,128)(2,1)}) custom-call(s32[2]{0:T(128)} %pad_add_fusion.core_ref, bf16[256,16384]{1,0:T(8,128)(2,1)} %get-tuple-element.107.refs_0_, f32[16,512,128]{2,1,0:T(8,128)} %get-tuple-element.108.refs_1_, ...), custom_call_target="tpu_custom_call", output_to_operand_aliasing={{0}: (1, {})} | custom-call | tf_op jit(solution)/shard_map/state_correction/pallas_call | solution.py:422
  515.3 23.6 %state_correction.5 = (bf16[256,16384]{1,0:T(8,128)(2,1)}, bf16[256,2048]{1,0:T(8,128)(2,1)}) custom-call(s32[2]{0:T(128)} %pad_add_fusion.core_ref, bf16[256,16384]{1,0:T(8,128)(2,1)} %get-tuple-element.112.refs_0_, f32[16,512,128]{2,1,0:T(8,128)} %get-tuple-element.113.refs_1_, ...), custom_call_target="tpu_custom_call", output_to_operand_aliasing={{0}: (1, {})} | custom-call | tf_op jit(solution)/shard_map/state_correction/pallas_call | solution.py:422
  539.5 4.5 place_channels.3.buffer_ref
  543.9 1.0 copy-done.9
  544.9 2.7 place_channels.4.buffer_ref
  547.6 2.7 place_channels.5
  550.3 1.6 copy.55
  (119 shorter events, 11.5 us)
Async XLA Ops:
  7.2 279.1 %all-gather.3.cloned.1.call-start = ((), (), s32[]{:S(2)}) async-start(), calls=%async_computation.8 | async-start | bytes 4456448 | tf_op jit(solution)/shard_map/all_gather | solution.py:561
  9.1 46.2 %collective-permute-start.2 = (bf16[128,1024]{1,0:T(8,128)(2,1)}, bf16[128,1024]{1,0:T(8,128)(2,1)}, u32[]{:S(2)}, u32[]{:S(2)}) collective-permute-start(bf16[128,1024]{1,0:T(8,128)(2,1)} %get-tuple-element.123), channel_id=1, source_target_pairs={{0,6},{2,0},{4,2},{6,4},{1,7},{3,1},{5,3},{7,5},{8,14},{10,8},{12,... | collective-permute-start | bytes 786440 | tf_op jit(solution)/shard_map/ppermute | solution.py:559
  14.2 41.4 %collective-permute-start.1 = (bf16[128,1024]{1,0:T(8,128)(2,1)}, bf16[128,1024]{1,0:T(8,128)(2,1)}, u32[]{:S(2)}, u32[]{:S(2)}) collective-permute-start(bf16[128,1024]{1,0:T(8,128)(2,1)} %get-tuple-element.123), channel_id=1, source_target_pairs={{0,4},{2,6},{4,0},{6,2},{1,5},{3,7},{5,1},{7,3},{8,12},{10,14},{12... | collective-permute-start | bytes 786440 | tf_op jit(solution)/shard_map/ppermute | solution.py:559
  14.2 41.7 %collective-permute-start = (bf16[128,1024]{1,0:T(8,128)(2,1)}, bf16[128,1024]{1,0:T(8,128)(2,1)}, u32[]{:S(2)}, u32[]{:S(2)}) collective-permute-start(bf16[128,1024]{1,0:T(8,128)(2,1)} %get-tuple-element.123), channel_id=1, source_target_pairs={{0,2},{2,4},{4,6},{6,0},{1,3},{3,5},{5,7},{7,1},{8,10},{10,12},{12... | collective-permute-start | bytes 786440 | tf_op jit(solution)/shard_map/ppermute | solution.py:559
  16.5 10.5 %collective-permute-start.3 = (bf16[3,8192]{1,0:T(4,128)(2,1)S(1)}, bf16[3,8192]{1,0:T(4,128)(2,1)S(1)}, u32[]{:S(2)}, u32[]{:S(2)}) collective-permute-start(bf16[3,8192]{1,0:T(4,128)(2,1)S(1)} %reshape.115), channel_id=1, source_target_pairs={{0,1},{1,0},{2,3},{3,2},{4,5},{5,4},{6,7},{7,6},{8,9},{9,8},{10,11... | collective-permute-start | bytes 147464 | tf_op jit(solution)/shard_map/ppermute | solution.py:595
  21.7 135.1 %collective-permute-start.4 = (bf16[256,4096]{1,0:T(8,128)(2,1)}, bf16[256,4096]{1,0:T(8,128)(2,1)}, u32[]{:S(2)}, u32[]{:S(2)}) collective-permute-start(bf16[256,4096]{1,0:T(8,128)(2,1)} %pick_channels.4), channel_id=1, source_target_pairs={{0,1},{1,0},{2,3},{3,2},{4,5},{5,4},{6,7},{7,6},{8,9},{9,8},{10,11... | collective-permute-start | bytes 6291464 | tf_op jit(solution)/shard_map/ppermute | solution.py:653
  22.2 4.7 copy-start.26
  27.0 129.8 %collective-permute-start.5 = (bf16[256,4096]{1,0:T(8,128)(2,1)}, bf16[256,4096]{1,0:T(8,128)(2,1)S(1)}, u32[]{:S(2)}, u32[]{:S(2)}) collective-permute-start(bf16[256,4096]{1,0:T(8,128)(2,1)} %pick_channels.5), channel_id=1, source_target_pairs={{0,1},{1,0},{2,3},{3,2},{4,5},{5,4},{6,7},{7,6},{8,9},{9,8},{10,11... | collective-permute-start | bytes 6291464 | tf_op jit(solution)/shard_map/ppermute | solution.py:653
  28.5 49.4 %all-to-all-start = ((bf16[16,3,8192]{2,1,0:T(4,128)(2,1)}), bf16[16,3,8192]{2,1,0:T(4,128)(2,1)S(1)}, u32[]{:S(2)}, u32[]{:S(2)}) async-start(bf16[16,3,8192]{2,1,0:T(4,128)(2,1)} %broadcast_in_dim.125), calls=%async_computation | async-start | bytes 2097152 | tf_op jit(solution)/shard_map/all_to_all | solution.py:597
  36.8 6.2 %copy-start.24 = (s32[16]{0:T(128)}, s32[16]{0:T(128)S(1)}, u32[]{:S(2)}) copy-start(s32[16]{0:T(128)S(1)} %get-tuple-element.121) | copy-start | bytes 196
  47.5 4.8 copy-start.4
  55.3 31.9 %collective-permute-start.6 = (bf16[256,32]{0,1:T(8,128)(2,1)}, bf16[256,32]{0,1:T(8,128)(2,1)}, u32[]{:S(2)}, u32[]{:S(2)}) collective-permute-start(bf16[256,32]{0,1:T(8,128)(2,1)} %param.17), channel_id=1, source_target_pairs={{0,1},{1,0},{2,3},{3,2},{4,5},{5,4},{6,7},{7,6},{8,9},{9,8},{10,11... | collective-permute-start | bytes 49160 | tf_op jit(solution)/shard_map/ppermute | solution.py:638
  55.5 101.3 %collective-permute-start.11 = (bf16[256,4096]{1,0:T(8,128)(2,1)}, bf16[256,4096]{1,0:T(8,128)(2,1)}, u32[]{:S(2)}, u32[]{:S(2)}) collective-permute-start(bf16[256,4096]{1,0:T(8,128)(2,1)} %pick_channels.6), channel_id=1, source_target_pairs={{0,1},{1,0},{2,3},{3,2},{4,5},{5,4},{6,7},{7,6},{8,9},{9,8},{10,11... | collective-permute-start | bytes 6291464 | tf_op jit(solution)/shard_map/ppermute | solution.py:634
  55.8 101.0 %collective-permute-start.12 = (bf16[256,4096]{1,0:T(8,128)(2,1)}, bf16[256,4096]{1,0:T(8,128)(2,1)}, u32[]{:S(2)}, u32[]{:S(2)}) collective-permute-start(bf16[256,4096]{1,0:T(8,128)(2,1)} %pick_channels.7), channel_id=1, source_target_pairs={{0,1},{1,0},{2,3},{3,2},{4,5},{5,4},{6,7},{7,6},{8,9},{9,8},{10,11... | collective-permute-start | bytes 6291464 | tf_op jit(solution)/shard_map/ppermute | solution.py:634
  58.4 28.7 %copy-start.19 = (bf16[4,2048]{1,0:T(4,128)(2,1)S(1)}, bf16[4,2048]{1,0:T(4,128)(2,1)}, u32[]{:S(2)}) copy-start(bf16[4,2048]{1,0:T(4,128)(2,1)} %param.18) | copy-start | bytes 49156
  79.5 5.1 copy-start.25
  79.5 5.7 %copy-start.23 = (s32[512]{0:T(512)S(1)}, s32[512]{0:T(512)}, u32[]{:S(2)}) copy-start(s32[512]{0:T(512)} %add_select_fusion) | copy-start | bytes 6148
  79.5 7.6 %copy-start.17 = (f32[16,2048]{1,0:T(8,128)S(1)}, f32[16,2048]{1,0:T(8,128)}, u32[]{:S(2)}) copy-start(f32[16,2048]{1,0:T(8,128)} %param.22) | copy-start | bytes 393220
  79.5 7.6 %copy-start.20 = (f32[2048]{0:T(1024)S(1)}, f32[2048]{0:T(1024)}, u32[]{:S(2)}) copy-start(f32[2048]{0:T(1024)} %param.19) | copy-start | bytes 24580
  79.5 7.6 %copy-start.21 = (f32[2048]{0:T(1024)S(1)}, f32[2048]{0:T(1024)}, u32[]{:S(2)}) copy-start(f32[2048]{0:T(1024)} %param.21) | copy-start | bytes 24580
  79.5 7.6 %copy-start.22 = (f32[2048]{0:T(1024)S(1)}, f32[2048]{0:T(1024)}, u32[]{:S(2)}) copy-start(f32[2048]{0:T(1024)} %param.23) | copy-start | bytes 24580
  80.3 74.2 %all-to-all-start.1 = ((bf16[256,8,256]{0,2,1:T(8,128)(2,1)}), bf16[256,8,256]{0,2,1:T(8,128)(2,1)}, u32[]{:S(2)}, u32[]{:S(2)}) async-start(bf16[256,8,256]{0,2,1:T(8,128)(2,1)} %bitcast.15), calls=%async_computation.1 | async-start | bytes 2097152 | tf_op jit(solution)/shard_map/all_to_all | solution.py:620
  87.2 63.6 %copy-start.13 = (f32[24,2048]{1,0:T(8,128)}, f32[24,2048]{1,0:T(8,128)S(1)}, u32[]{:S(2)}) copy-start(f32[24,2048]{1,0:T(8,128)S(1)} %concatenate.24) | copy-start | bytes 589828
  87.2 37.7 %collective-permute-start.9 = (f32[24,2048]{1,0:T(8,128)S(1)}, f32[24,2048]{1,0:T(8,128)S(1)}, u32[]{:S(2)}, u32[]{:S(2)}) collective-permute-start(f32[24,2048]{1,0:T(8,128)S(1)} %concatenate.24), channel_id=1, source_target_pairs={{0,6},{2,0},{4,2},{6,4},{1,7},{3,1},{5,3},{7,5},{8,14},{10,8},{12,... | collective-permute-start | bytes 589832 | tf_op jit(solution)/shard_map/ppermute | solution.py:657
  124.9 25.8 %copy-start.15 = (f32[24,2048]{1,0:T(8,128)}, f32[24,2048]{1,0:T(8,128)S(1)}, u32[]{:S(2)}) copy-start(f32[24,2048]{1,0:T(8,128)S(1)} %collective-permute-done.9) | copy-start | bytes 589828
  124.9 17.5 %collective-permute-start.8 = (f32[24,2048]{1,0:T(8,128)S(1)}, f32[24,2048]{1,0:T(8,128)S(1)}, u32[]{:S(2)}, u32[]{:S(2)}) collective-permute-start(f32[24,2048]{1,0:T(8,128)S(1)} %concatenate.24), channel_id=1, source_target_pairs={{0,4},{2,6},{4,0},{6,2},{1,5},{3,7},{5,1},{7,3},{8,12},{10,14},{12... | collective-permute-start | bytes 589832 | tf_op jit(solution)/shard_map/ppermute | solution.py:657
  142.4 8.3 %copy-start.16 = (f32[24,2048]{1,0:T(8,128)}, f32[24,2048]{1,0:T(8,128)S(1)}, u32[]{:S(2)}) copy-start(f32[24,2048]{1,0:T(8,128)S(1)} %collective-permute-done.8) | copy-start | bytes 589828
  142.4 8.3 %collective-permute-start.7 = (f32[24,2048]{1,0:T(8,128)S(1)}, f32[24,2048]{1,0:T(8,128)S(1)}, u32[]{:S(2)}, u32[]{:S(2)}) collective-permute-start(f32[24,2048]{1,0:T(8,128)S(1)} %concatenate.24), channel_id=1, source_target_pairs={{0,2},{2,4},{4,6},{6,0},{1,3},{3,5},{5,7},{7,1},{8,10},{10,12},{12... | collective-permute-start | bytes 589832 | tf_op jit(solution)/shard_map/ppermute | solution.py:657
  150.7 1.9 collective-permute-start.10
  151.9 8.4 %copy-start = (f32[4,24,2048]{2,1,0:T(8,128)}, f32[4,24,2048]{2,1,0:T(8,128)S(1)}, u32[]{:S(2)}) copy-start(f32[4,24,2048]{2,1,0:T(8,128)S(1)} %pad_maximum_fusion.2.param_ref.refs_3_.refs_4_) | copy-start | bytes 2359300
  152.6 7.7 %copy-start.5 = (bf16[256,512]{1,0:T(8,128)(2,1)}, bf16[256,512]{1,0:T(8,128)(2,1)S(1)}, u32[]{:S(2)}) copy-start(bf16[256,512]{1,0:T(8,128)(2,1)S(1)} %collective-permute-done.10.low_other_ref) | copy-start | bytes 786436
  156.8 3.6 copy-start.1
  156.8 3.6 copy-start.6
  161.9 3.8 copy-start.3
  161.9 33.3 %copy-start.12 = (bf16[512,16,16]{0,2,1:T(8,128)(2,1)S(1)}, bf16[512,16,16]{0,2,1:T(8,128)(2,1)}, u32[]{:S(2)}) copy-start(bf16[512,16,16]{0,2,1:T(8,128)(2,1)} %broadcast_select_fusion) | copy-start | bytes 786436
  161.9 118.3 %all-to-all-start.2 = ((bf16[256,8,512]{2,0,1:T(8,128)(2,1)}), bf16[256,8,512]{2,0,1:T(8,128)(2,1)S(1)}, u32[]{:S(2)}, u32[]{:S(2)}) async-start(bf16[256,8,512]{2,0,1:T(8,128)(2,1)} %bitcast.58), calls=%async_computation.2 | async-start | bytes 4194304 | tf_op jit(solution)/shard_map/all_to_all | solution.py:701
  165.7 26.1 %collective-permute-start.13 = (bf16[4,128,1024]{2,1,0:T(8,128)(2,1)S(1)}, bf16[4,128,1024]{2,1,0:T(8,128)(2,1)S(1)}, u32[]{:S(2)}, u32[]{:S(2)}) collective-permute-start(bf16[4,128,1024]{2,1,0:T(8,128)(2,1)S(1)} %copy-done.3), channel_id=1, source_target_pairs={{0,8},{8,0},{16,24},{24,16},{1,9},{9,1},{17,25},{25,17},{2,10},{10... | collective-permute-start | bytes 3145736 | tf_op jit(solution)/shard_map/ppermute | solution.py:618
  167.3 48.6 %collective-permute-start.14 = (bf16[4,128,1024]{2,1,0:T(8,128)(2,1)S(1)}, bf16[4,128,1024]{2,1,0:T(8,128)(2,1)}, u32[]{:S(2)}, u32[]{:S(2)}) collective-permute-start(bf16[4,128,1024]{2,1,0:T(8,128)(2,1)S(1)} %copy-done.3), channel_id=1, source_target_pairs={{0,16},{8,24},{16,0},{24,8},{1,17},{9,25},{17,1},{25,9},{2,18},{10... | collective-permute-start | bytes 3145736 | tf_op jit(solution)/shard_map/ppermute | solution.py:618
  168.7 47.1 %collective-permute-start.15 = (bf16[4,128,1024]{2,1,0:T(8,128)(2,1)S(1)}, bf16[4,128,1024]{2,1,0:T(8,128)(2,1)}, u32[]{:S(2)}, u32[]{:S(2)}) collective-permute-start(bf16[4,128,1024]{2,1,0:T(8,128)(2,1)S(1)} %copy-done.3), channel_id=1, source_target_pairs={{0,24},{8,16},{16,8},{24,0},{1,25},{9,17},{17,9},{25,1},{2,26},{10... | collective-permute-start | bytes 3145736 | tf_op jit(solution)/shard_map/ppermute | solution.py:618
  169.2 111.0 %collective-permute-start.16 = (bf16[2048,256]{1,0:T(8,128)(2,1)}, bf16[2048,256]{1,0:T(8,128)(2,1)}, u32[]{:S(2)}, u32[]{:S(2)}) collective-permute-start(bf16[2048,256]{1,0:T(8,128)(2,1)} %bitcast.59), channel_id=1, source_target_pairs={{0,8},{8,0},{16,24},{24,16},{1,9},{9,1},{17,25},{25,17},{2,10},{10... | collective-permute-start | bytes 3145736 | tf_op jit(solution)/shard_map/ppermute | solution.py:702
  170.7 109.5 %collective-permute-start.17 = (bf16[2048,256]{1,0:T(8,128)(2,1)}, bf16[2048,256]{1,0:T(8,128)(2,1)}, u32[]{:S(2)}, u32[]{:S(2)}) collective-permute-start(bf16[2048,256]{1,0:T(8,128)(2,1)} %bitcast.60), channel_id=1, source_target_pairs={{0,16},{8,24},{16,0},{24,8},{1,17},{9,25},{17,1},{25,9},{2,18},{10... | collective-permute-start | bytes 3145736 | tf_op jit(solution)/shard_map/ppermute | solution.py:702
  191.7 1.0 copy-start.8
  192.8 87.5 %collective-permute-start.18 = (bf16[2048,256]{1,0:T(8,128)(2,1)}, bf16[2048,256]{1,0:T(8,128)(2,1)}, u32[]{:S(2)}, u32[]{:S(2)}) collective-permute-start(bf16[2048,256]{1,0:T(8,128)(2,1)} %bitcast.61), channel_id=1, source_target_pairs={{0,24},{8,16},{16,8},{24,0},{1,25},{9,17},{17,9},{25,1},{2,26},{10... | collective-permute-start | bytes 3145736 | tf_op jit(solution)/shard_map/ppermute | solution.py:702
  280.3 40.8 %copy-start.2 = (bf16[256,8,512]{2,0,1:T(8,128)(2,1)}, bf16[256,8,512]{2,0,1:T(8,128)(2,1)S(1)}, u32[]{:S(2)}) copy-start(bf16[256,8,512]{2,0,1:T(8,128)(2,1)S(1)} %all-to-all-done.2) | copy-start | bytes 6291460
  280.3 40.8 %all-to-all-start.3 = ((bf16[16,32,256]{2,1,0:T(8,128)(2,1)}), bf16[16,32,256]{2,1,0:T(8,128)(2,1)S(1)}, u32[]{:S(2)}, u32[]{:S(2)}) async-start(bf16[16,32,256]{2,1,0:T(8,128)(2,1)} %get-tuple-element.80), calls=%async_computation.3 | async-start | bytes 524288 | tf_op jit(solution)/shard_map/all_to_all | solution.py:680
  321.1 0.7 copy-start.11
  324.3 43.5 %all-to-all-start.4 = ((bf16[16,16,256]{2,1,0:T(8,128)(2,1)}), bf16[16,16,256]{2,1,0:T(8,128)(2,1)S(1)}, u32[]{:S(2)}, u32[]{:S(2)}) async-start(bf16[16,16,256]{2,1,0:T(8,128)(2,1)} %state_combine.2), calls=%async_computation.4 | async-start | bytes 262144 | tf_op jit(solution)/shard_map/all_to_all | solution.py:680
  331.2 35.0 %copy-start.18 = (bf16[8,32,256]{2,1,0:T(8,128)(2,1)S(1)}, bf16[8,32,256]{2,1,0:T(8,128)(2,1)}, u32[]{:S(2)}) copy-start(bf16[8,32,256]{2,1,0:T(8,128)(2,1)} %get-tuple-element.84) | copy-start | bytes 393220
  367.8 65.2 %copy-start.14 = (bf16[16,16,256]{2,1,0:T(8,128)(2,1)}, bf16[16,16,256]{2,1,0:T(8,128)(2,1)S(1)}, u32[]{:S(2)}) copy-start(bf16[16,16,256]{2,1,0:T(8,128)(2,1)S(1)} %all-to-all-done.4.refs_2_) | copy-start | bytes 393220
  367.8 65.2 %all-to-all-start.5 = ((bf16[16,32,256]{2,1,0:T(8,128)(2,1)}), bf16[16,32,256]{2,1,0:T(8,128)(2,1)S(1)}, u32[]{:S(2)}, u32[]{:S(2)}) async-start(bf16[16,32,256]{2,1,0:T(8,128)(2,1)} %pad_maximum_fusion.5), calls=%async_computation.5 | async-start | bytes 524288 | tf_op jit(solution)/shard_map/all_to_all | solution.py:680
  433.0 0.7 copy-start.10
  436.2 49.3 %all-to-all-start.6 = ((bf16[16,16,256]{2,1,0:T(8,128)(2,1)}), bf16[16,16,256]{2,1,0:T(8,128)(2,1)S(1)}, u32[]{:S(2)}, u32[]{:S(2)}) async-start(bf16[16,16,256]{2,1,0:T(8,128)(2,1)} %state_combine.3), calls=%async_computation.6 | async-start | bytes 262144 | tf_op jit(solution)/shard_map/all_to_all | solution.py:680
  485.6 0.7 copy-start.7
  486.2 64.1 %all-to-all-start.7 = ((bf16[8,256,512]{2,1,0:T(8,128)(2,1)}), bf16[8,256,512]{2,1,0:T(8,128)(2,1)S(1)}, u32[]{:S(2)}, u32[]{:S(2)}) async-start(bf16[8,256,512]{2,1,0:T(8,128)(2,1)} %bitcast.33), calls=%async_computation.7 | async-start | bytes 4194304 | tf_op jit(solution)/shard_map/all_to_all | solution.py:722
  491.2 48.2 %collective-permute-start.19 = (bf16[256,4096]{1,0:T(8,128)(2,1)}, bf16[256,4096]{1,0:T(8,128)(2,1)}, u32[]{:S(2)}, u32[]{:S(2)}) collective-permute-start(bf16[256,4096]{1,0:T(8,128)(2,1)} %get-tuple-element.116), channel_id=1, source_target_pairs={{0,1},{1,0},{2,3},{3,2},{4,5},{5,4},{6,7},{7,6},{8,9},{9,8},{10,11... | collective-permute-start | bytes 6291464 | tf_op jit(solution)/shard_map/ppermute | solution.py:721
  515.3 28.6 %collective-permute-start.20 = (bf16[256,2048]{1,0:T(8,128)(2,1)}, bf16[256,2048]{1,0:T(8,128)(2,1)S(1)}, u32[]{:S(2)}, u32[]{:S(2)}) collective-permute-start(bf16[256,2048]{1,0:T(8,128)(2,1)} %get-tuple-element.117), channel_id=1, source_target_pairs={{0,1},{1,0},{2,3},{3,2},{4,5},{5,4},{6,7},{7,6},{8,9},{9,8},{10,11... | collective-permute-start | bytes 3145736 | tf_op jit(solution)/shard_map/ppermute | solution.py:724
  539.0 8.6 %collective-permute-start.21 = (bf16[256,2048]{1,0:T(8,128)(2,1)}, bf16[256,2048]{1,0:T(8,128)(2,1)}, u32[]{:S(2)}, u32[]{:S(2)}) collective-permute-start(bf16[256,2048]{1,0:T(8,128)(2,1)} %get-tuple-element.118), channel_id=1, source_target_pairs={{0,1},{1,0},{2,3},{3,2},{4,5},{5,4},{6,7},{7,6},{8,9},{9,8},{10,11... | collective-permute-start | bytes 3145736 | tf_op jit(solution)/shard_map/ppermute | solution.py:726
  543.9 1.0 copy-start.9
Sparse Core Ops, SparseCore 0:
  22.3 105.4 all-gather.2

commit v2 on v1

--- a/solution.py
+++ b/solution.py
@@ -160,7 +160,7 @@
 
     zero = jnp.zeros((8, tiles[0].stop), jnp.float32)
     lax.fori_loop(0, tokens // GROUP, step16, (zero,) * len(tiles))
-    rows = 16
+    rows = 32
 
     def gated(gate_ref, dest_ref, offset):
         def body(step, carry):
@@ -558,8 +558,6 @@
     shards_first = jnp.stack(
         [part_first] + [lax.ppermute(part_first, "chip", move) for move in far_moves]
     )
-    weights_later = lax.all_gather(part_later, chips, axis=0, tiled=False)
-    weights_later = [weights_later.reshape(blk_count, chip_count, part_rows, width)]
 
     def by_flip(low):
         return jnp.concatenate(
@@ -613,10 +611,13 @@
     kv_rows = jnp.broadcast_to(
         kv_rows[:, :, None], (half, kv_heads, repeat, 2, HD)
     ).reshape(half, ulys_count * 2 * HD)
-    kv_rows, shards_first, halo = lax.optimization_barrier((kv_rows, shards_first, halo))
+    kv_rows, halo = lax.optimization_barrier((kv_rows, halo))
+    shards_first, part_later = lax.optimization_barrier((shards_first, part_later))
+    weights_later = lax.all_gather(part_later, chips, axis=0, tiled=False)
     weights_first = [shards_first] + [
         lax.ppermute(shards_first, "blk", move) for move in flips
     ]
+    weights_later = [weights_later.reshape(blk_count, chip_count, part_rows, width)]
     kv_local = lax.all_to_all(kv_rows, ulys, split_axis=1, concat_axis=0, tiled=True)
 
     packed = jnp.concatenate(
@@ -630,8 +631,12 @@
         ],
         axis=0,
     )
+
+    def picked(full, piece):
+        return run_pick(core_arr, full, piece, width)
+
     x_other = [
-        lax.ppermute(run_pick(core_arr, mamba_input, piece, width), "core", swap)
+        lax.ppermute(picked(mamba_input, piece), "core", swap)
         for piece in range(PIECES)
     ]
     low_other = lax.ppermute(delta_low, "core", swap)
@@ -650,7 +655,7 @@
     ).reshape(tokens, GROUP * STATE)
 
     gate_other = [
-        lax.ppermute(run_pick(core_arr, gate_input, piece, width), "core", swap)
+        lax.ppermute(picked(gate_input, piece), "core", swap)
         for piece in range(PIECES)
     ]
 

time: 561 us -> 568 us (1.012)
  waiting for transfers between devices: 107 us -> 120 us
    ppermute x3, waiting for transfers between devices: 0.01 us -> 19.8 us  [local(): lax.ppermute(part_first, 'chip', move)]
    all_to_all x1, waiting for transfers between devices: 19.5 us -> 7.51 us  [local(): lax.all_to_all(jnp.broadcast_to(tail[None], (chunks, CONV - 1, PIECES * c...]
  transfers between devices with their start and end apart: 31 -> 31, of which waited for: 6 -> 8; matrix products, arithmetic and copies ran while one was open for 7% -> 6% of each run, Pallas kernels for 55% -> 54%
where the time goes in v2:
time: 568 us; the launch traced here: 566 us
  Pallas kernels  314 us (55%)
  waiting for transfers between devices  120 us (21%)
  starting transfers between devices  73.5 us (13%)
  local copies, waits for them, and re-layouts  25.8 us (5%)
  other arithmetic  16.6 us (3%)
  between operations  15.8 us (3%)
    pallas_call x3, Pallas kernels, run_scan(): pl.pallas_call(functools.partial(scan_kernel, sources=sources), grid_spec...  134 us
    pallas_call x3, Pallas kernels, run_correct(): pl.pallas_call(functools.partial(correct_kernel, resumed=resumed), grid_s...  88.4 us
    pallas_call x1, Pallas kernels, run_flash(): pl.pallas_call(functools.partial(flash_kernel, heads=heads, rows=rows, so...  58.3 us
    ppermute x3, waiting for transfers between devices, local(): lax.ppermute(packed, 'chip', move)  49.9 us
    ppermute x3, waiting for transfers between devices, local(): lax.ppermute(shards_first, 'blk', move)  42.3 us
    all_to_all x4, starting transfers between devices, to_owners(): return lax.all_to_all(array, chips, split_axis=0, concat_axis=0, tiled=True)  27.2 us
    ppermute x3, waiting for transfers between devices, local(): lax.ppermute(part_first, 'chip', move)  19.8 us
    pallas_call x4, Pallas kernels, run_pick(): pl.pallas_call(copy_kernel, grid_spec=pltpu.PrefetchScalarGridSpec(num_sc...  17.9 us
  transfers between devices with their start and end apart: 31, of which 8 were waited for; matrix products, arithmetic and copies ran while one was open for 6% of the time, Pallas kernels for 54%

profile of v2, /device:TPU:0, one launch (start us, length us, event | category | flops | bytes accessed | tf_op | source)
XLA Modules:
  0.0 566.3 jit_solution(2099108015081820621)
XLA Ops:
  7.2 1.8 fusion.12
  9.0 5.1 collective-permute-start.12
  14.1 1.0 collective-permute-start.10
  15.1 1.0 slice.22
  16.6 4.2 collective-permute-done.12
  20.8 15.6 %collective-permute-done.11 = bf16[128,1024]{1,0:T(8,128)(2,1)S(1)} collective-permute-done((bf16[128,1024]{1,0:T(8,128)(2,1)S(1)}, bf16[128,1024]{1,0:T(8,128)(2,1)S(1)}, u32[]{:S(2)}, u32[]{:S(2)}) %collective-permute-start.11) | collective-permute-done | bytes 262176 | tf_op jit(solution)/shard_map/ppermute | solution.py:559
  36.4 1.1 pad_maximum_fusion.1.refs_0_
  37.6 1.4 broadcast_in_dim.125
  39.0 6.1 %all-to-all-start = ((bf16[16,3,8192]{2,1,0:T(4,128)(2,1)}), bf16[16,3,8192]{2,1,0:T(4,128)(2,1)S(1)}, u32[]{:S(2)}, u32[]{:S(2)}) async-start(bf16[16,3,8192]{2,1,0:T(4,128)(2,1)} %broadcast_in_dim.125), calls=%async_computation | async-start | bytes 2097152 | tf_op jit(solution)/shard_map/all_to_all | solution.py:595
  45.7 4.5 pick_channels.4
  50.1 4.5 pick_channels.5
  55.1 4.5 pick_channels.6
  60.1 4.5 pick_channels.7
  64.6 2.1 copy.39
  66.7 2.1 copy.38
  72.2 0.7 constant_dynamic-slice_fusion.7
  72.9 2.3 pad_maximum_fusion
  76.3 7.5 %all-to-all-done = bf16[16,3,8192]{2,1,0:T(4,128)(2,1)S(1)} async-done(((bf16[16,3,8192]{2,1,0:T(4,128)(2,1)}), bf16[16,3,8192]{2,1,0:T(4,128)(2,1)S(1)}, u32[]{:S(2)}, u32[]{:S(2)}) %all-to-all-start) | async-done | bytes 786464 | tf_op jit(solution)/shard_map/all_to_all | solution.py:595
  83.8 1.6 fusion
  86.3 4.2 all-to-all-start.1
  91.1 1.9 compare_convert_fusion
  93.2 3.8 collective-permute-start.6
  97.5 0.8 maximum_select_fusion
  98.3 34.9 %collective-permute-done.6 = f32[24,2048]{1,0:T(8,128)S(1)} collective-permute-done((f32[24,2048]{1,0:T(8,128)S(1)}, f32[24,2048]{1,0:T(8,128)S(1)}, u32[]{:S(2)}, u32[]{:S(2)}) %collective-permute-start.6) | collective-permute-done | bytes 196640 | tf_op jit(solution)/shard_map/ppermute | solution.py:662
  133.3 10.1 %collective-permute-start.5 = (f32[24,2048]{1,0:T(8,128)S(1)}, f32[24,2048]{1,0:T(8,128)S(1)}, u32[]{:S(2)}, u32[]{:S(2)}) collective-permute-start(f32[24,2048]{1,0:T(8,128)S(1)} %concatenate.24), channel_id=1, source_target_pairs={{0,4},{2,6},{4,0},{6,2},{1,5},{3,7},{5,1},{7,3},{8,12},{10,14},{12... | collective-permute-start | bytes 589832 | tf_op jit(solution)/shard_map/ppermute | solution.py:662
  143.5 0.7 reshape.117
  144.3 8.0 %collective-permute-done.5 = f32[24,2048]{1,0:T(8,128)S(1)} collective-permute-done((f32[24,2048]{1,0:T(8,128)S(1)}, f32[24,2048]{1,0:T(8,128)S(1)}, u32[]{:S(2)}, u32[]{:S(2)}) %collective-permute-start.5) | collective-permute-done | bytes 196640 | tf_op jit(solution)/shard_map/ppermute | solution.py:662
  152.8 0.8 broadcast_select_fusion
  153.5 7.0 %collective-permute-done.4 = f32[24,2048]{1,0:T(8,128)S(1)} collective-permute-done((f32[24,2048]{1,0:T(8,128)S(1)}, f32[24,2048]{1,0:T(8,128)S(1)}, u32[]{:S(2)}, u32[]{:S(2)}) %collective-permute-start.4) | collective-permute-done | bytes 196640 | tf_op jit(solution)/shard_map/ppermute | solution.py:662
  160.5 1.2 pad_maximum_fusion.2.param_ref.refs_3_.refs_4_
  161.7 0.7 multiply_bitcast_fusion
  162.5 1.8 pad_maximum_fusion.3
  164.3 2.3 copy.42
  166.6 3.5 broadcast_in_dim.128.inject_ref
  170.1 1.5 copy.62
  171.7 3.7 all-to-all-start.2
  175.5 0.8 collective-permute-start.14
  176.3 2.7 collective-permute-start.15
  179.1 0.7 collective-permute-start.17
  179.8 21.7 %collective-permute-done.13.refs_1_ = bf16[4,128,1024]{2,1,0:T(8,128)(2,1)S(1)} collective-permute-done((bf16[4,128,1024]{2,1,0:T(8,128)(2,1)S(1)}, bf16[4,128,1024]{2,1,0:T(8,128)(2,1)S(1)}, u32[]{:S(2)}, u32[]{:S(2)}) %collective-permute-start.13) | collective-permute-done | bytes 1048608 | tf_op jit(solution)/shard_map/ppermute | solution.py:618
  201.5 1.0 copy-done.8
  202.8 0.9 copy.44.read_ref.refs_4_.refs_5_
  203.7 20.5 %collective-permute-done.14.refs_2_ = bf16[4,128,1024]{2,1,0:T(8,128)(2,1)} collective-permute-done((bf16[4,128,1024]{2,1,0:T(8,128)(2,1)S(1)}, bf16[4,128,1024]{2,1,0:T(8,128)(2,1)}, u32[]{:S(2)}, u32[]{:S(2)}) %collective-permute-start.14) | collective-permute-done | bytes 1048608 | tf_op jit(solution)/shard_map/ppermute | solution.py:618
  224.2 64.3 %token_scan.3 = (f32[32,512,128]{2,1,0:T(8,128)}, bf16[512,4096]{1,0:T(8,128)(2,1)}, bf16[16,32,256]{2,1,0:T(8,128)(2,1)}) custom-call(s32[2]{0:T(128)} %pad_add_fusion.core_ref, bf16[256,16384]{1,0:T(8,128)(2,1)} %own_ref.5, bf16[256,4096]{1,0:T(8,128)(2,1)} %collective-permute-done.8.other_ref, bf16[8,8192]{1,0:T(8,128)(2,1)} %concatenate.21.halo_ref, ...), custom_call_target="tpu_custom_call" | custom-call | tf_op jit(solution)/shard_map/token_scan/pallas_call | solution.py:370
  288.6 6.5 %all-to-all-start.3 = ((bf16[16,32,256]{2,1,0:T(8,128)(2,1)}), bf16[16,32,256]{2,1,0:T(8,128)(2,1)S(1)}, u32[]{:S(2)}, u32[]{:S(2)}) async-start(bf16[16,32,256]{2,1,0:T(8,128)(2,1)} %get-tuple-element.81), calls=%async_computation.3 | async-start | bytes 524288 | tf_op jit(solution)/shard_map/all_to_all | solution.py:685
  295.1 34.8 %token_scan.4 = (f32[16,512,128]{2,1,0:T(8,128)}, bf16[512,2048]{1,0:T(8,128)(2,1)}, bf16[8,32,256]{2,1,0:T(8,128)(2,1)}) custom-call(s32[2]{0:T(128)} %pad_add_fusion.core_ref, bf16[256,16384]{1,0:T(8,128)(2,1)} %own_ref.5, bf16[256,4096]{1,0:T(8,128)(2,1)} %collective-permute-done.9.other_ref, bf16[8,8192]{1,0:T(8,128)(2,1)} %concatenate.21.halo_ref, ...), custom_call_target="tpu_custom_call" | custom-call | tf_op jit(solution)/shard_map/token_scan/pallas_call | solution.py:370
  329.9 0.7 copy-done.11
  330.6 2.5 state_combine.2
  333.1 6.9 %all-to-all-start.4 = ((bf16[16,16,256]{2,1,0:T(8,128)(2,1)}), bf16[16,16,256]{2,1,0:T(8,128)(2,1)S(1)}, u32[]{:S(2)}, u32[]{:S(2)}) async-start(bf16[16,16,256]{2,1,0:T(8,128)(2,1)} %state_combine.2), calls=%async_computation.4 | async-start | bytes 262144 | tf_op jit(solution)/shard_map/all_to_all | solution.py:685
  340.1 35.0 %token_scan.5 = (f32[16,512,128]{2,1,0:T(8,128)}, bf16[512,2048]{1,0:T(8,128)(2,1)}, bf16[8,32,256]{2,1,0:T(8,128)(2,1)}) custom-call(s32[2]{0:T(128)} %pad_add_fusion.core_ref, bf16[256,16384]{1,0:T(8,128)(2,1)} %own_ref.5, bf16[256,4096]{1,0:T(8,128)(2,1)} %collective-permute-done.9.other_ref, bf16[8,8192]{1,0:T(8,128)(2,1)} %concatenate.21.halo_ref, ...), custom_call_target="tpu_custom_call" | custom-call | tf_op jit(solution)/shard_map/token_scan/pallas_call | solution.py:370
  375.0 1.6 pad_maximum_fusion.5
  376.6 6.9 %all-to-all-start.5 = ((bf16[16,32,256]{2,1,0:T(8,128)(2,1)}), bf16[16,32,256]{2,1,0:T(8,128)(2,1)S(1)}, u32[]{:S(2)}, u32[]{:S(2)}) async-start(bf16[16,32,256]{2,1,0:T(8,128)(2,1)} %pad_maximum_fusion.5), calls=%async_computation.5 | async-start | bytes 524288 | tf_op jit(solution)/shard_map/all_to_all | solution.py:685
  383.6 58.3 %causal_attention.1 = bf16[2048,512]{1,0:T(8,128)(2,1)} custom-call(s32[9]{0:T(128)} %compare_convert_fusion.2.side_ref, s32[9]{0:T(128)} %get-tuple-element.93.flip_ref, s32[9]{0:T(128)} %get-tuple-element.94.half_ref, s32[9]{0:T(128)} %get-tuple-element.97.diag_ref.last_ref, s32[9]{0:T(128)} %get-tuple-element.96.first_ref, ...), custom_call_target="tpu_custom_call" | custom-call | tf_op jit(solution)/shard_map/causal_attention/pallas_call | solution.py:489
  442.5 2.5 state_combine.3
  445.1 6.9 %all-to-all-start.6 = ((bf16[16,16,256]{2,1,0:T(8,128)(2,1)}), bf16[16,16,256]{2,1,0:T(8,128)(2,1)S(1)}, u32[]{:S(2)}, u32[]{:S(2)}) async-start(bf16[16,16,256]{2,1,0:T(8,128)(2,1)} %state_combine.3), calls=%async_computation.6 | async-start | bytes 262144 | tf_op jit(solution)/shard_map/all_to_all | solution.py:685
  452.0 41.8 %state_correction.3 = (bf16[256,16384]{1,0:T(8,128)(2,1)}, bf16[256,4096]{1,0:T(8,128)(2,1)}) custom-call(s32[2]{0:T(128)} %pad_add_fusion.core_ref, f32[32,512,128]{2,1,0:T(8,128)} %get-tuple-element.71.refs_0_, bf16[512,4096]{1,0:T(8,128)(2,1)} %get-tuple-element.72.refs_1_, bf16[16,16,256]{2,1,0:T(8,128)(2,1)} %copy-done.14, f32[4,24,2048]{2,1,0:T(8,128)} %copy-done, ...), custom_call_target="tpu_custom_call" | custom-call | tf_op jit(solution)/shard_map/state_correction/pallas_call | solution.py:422
  494.4 5.0 all-to-all-start.7
  499.9 23.3 %state_correction.4 = (bf16[256,16384]{1,0:T(8,128)(2,1)}, bf16[256,2048]{1,0:T(8,128)(2,1)}) custom-call(s32[2]{0:T(128)} %pad_add_fusion.core_ref, bf16[256,16384]{1,0:T(8,128)(2,1)} %get-tuple-element.109.refs_0_, f32[16,512,128]{2,1,0:T(8,128)} %get-tuple-element.110.refs_1_, ...), custom_call_target="tpu_custom_call", output_to_operand_aliasing={{0}: (1, {})} | custom-call | tf_op jit(solution)/shard_map/state_correction/pallas_call | solution.py:422
  523.2 23.3 %state_correction.5 = (bf16[256,16384]{1,0:T(8,128)(2,1)}, bf16[256,2048]{1,0:T(8,128)(2,1)}) custom-call(s32[2]{0:T(128)} %pad_add_fusion.core_ref, bf16[256,16384]{1,0:T(8,128)(2,1)} %get-tuple-element.114.refs_0_, f32[16,512,128]{2,1,0:T(8,128)} %get-tuple-element.115.refs_1_, ...), custom_call_target="tpu_custom_call", output_to_operand_aliasing={{0}: (1, {})} | custom-call | tf_op jit(solution)/shard_map/state_correction/pallas_call | solution.py:422
  547.0 4.5 place_channels.3.buffer_ref
  551.5 1.0 copy-done.9
  552.4 2.7 place_channels.4.buffer_ref
  555.2 2.7 place_channels.5
  557.9 1.6 copy.55
  (119 shorter events, 11.1 us)
Async XLA Ops:
  7.2 287.9 %all-gather.3.cloned.1.call-start = ((), (), s32[]{:S(2)}) async-start(), calls=%async_computation.8 | async-start | bytes 4456448 | tf_op jit(solution)/shard_map/all_gather | solution.py:616
  9.0 11.8 %collective-permute-start.12 = (bf16[128,1024]{1,0:T(8,128)(2,1)S(1)}, bf16[128,1024]{1,0:T(8,128)(2,1)S(1)}, u32[]{:S(2)}, u32[]{:S(2)}) collective-permute-start(bf16[128,1024]{1,0:T(8,128)(2,1)S(1)} %get-tuple-element.125), channel_id=1, source_target_pairs={{0,6},{2,0},{4,2},{6,4},{1,7},{3,1},{5,3},{7,5},{8,14},{10,8},{12,... | collective-permute-start | bytes 786440 | tf_op jit(solution)/shard_map/ppermute | solution.py:559
  14.1 22.3 %collective-permute-start.11 = (bf16[128,1024]{1,0:T(8,128)(2,1)S(1)}, bf16[128,1024]{1,0:T(8,128)(2,1)S(1)}, u32[]{:S(2)}, u32[]{:S(2)}) collective-permute-start(bf16[128,1024]{1,0:T(8,128)(2,1)S(1)} %get-tuple-element.125), channel_id=1, source_target_pairs={{0,4},{2,6},{4,0},{6,2},{1,5},{3,7},{5,1},{7,3},{8,12},{10,14},{12... | collective-permute-start | bytes 786440 | tf_op jit(solution)/shard_map/ppermute | solution.py:559
  14.1 22.3 %collective-permute-start.10 = (bf16[128,1024]{1,0:T(8,128)(2,1)S(1)}, bf16[128,1024]{1,0:T(8,128)(2,1)S(1)}, u32[]{:S(2)}, u32[]{:S(2)}) collective-permute-start(bf16[128,1024]{1,0:T(8,128)(2,1)S(1)} %get-tuple-element.125), channel_id=1, source_target_pairs={{0,2},{2,4},{4,6},{6,0},{1,3},{3,5},{5,7},{7,1},{8,10},{10,12},{12... | collective-permute-start | bytes 786440 | tf_op jit(solution)/shard_map/ppermute | solution.py:559
  16.4 21.1 %collective-permute-start = (bf16[3,8192]{1,0:T(4,128)(2,1)S(1)}, bf16[3,8192]{1,0:T(4,128)(2,1)S(1)}, u32[]{:S(2)}, u32[]{:S(2)}) collective-permute-start(bf16[3,8192]{1,0:T(4,128)(2,1)S(1)} %reshape.115), channel_id=1, source_target_pairs={{0,1},{1,0},{2,3},{3,2},{4,5},{5,4},{6,7},{7,6},{8,9},{9,8},{10,11... | collective-permute-start | bytes 147464 | tf_op jit(solution)/shard_map/ppermute | solution.py:593
  39.0 44.8 %all-to-all-start = ((bf16[16,3,8192]{2,1,0:T(4,128)(2,1)}), bf16[16,3,8192]{2,1,0:T(4,128)(2,1)S(1)}, u32[]{:S(2)}, u32[]{:S(2)}) async-start(bf16[16,3,8192]{2,1,0:T(4,128)(2,1)} %broadcast_in_dim.125), calls=%async_computation | async-start | bytes 2097152 | tf_op jit(solution)/shard_map/all_to_all | solution.py:595
  50.1 116.4 %collective-permute-start.1 = (bf16[256,4096]{1,0:T(8,128)(2,1)}, bf16[256,4096]{1,0:T(8,128)(2,1)}, u32[]{:S(2)}, u32[]{:S(2)}) collective-permute-start(bf16[256,4096]{1,0:T(8,128)(2,1)} %pick_channels.4), channel_id=1, source_target_pairs={{0,1},{1,0},{2,3},{3,2},{4,5},{5,4},{6,7},{7,6},{8,9},{9,8},{10,11... | collective-permute-start | bytes 6291464 | tf_op jit(solution)/shard_map/ppermute | solution.py:658
  54.6 111.9 %collective-permute-start.2 = (bf16[256,4096]{1,0:T(8,128)(2,1)}, bf16[256,4096]{1,0:T(8,128)(2,1)S(1)}, u32[]{:S(2)}, u32[]{:S(2)}) collective-permute-start(bf16[256,4096]{1,0:T(8,128)(2,1)} %pick_channels.5), channel_id=1, source_target_pairs={{0,1},{1,0},{2,3},{3,2},{4,5},{5,4},{6,7},{7,6},{8,9},{9,8},{10,11... | collective-permute-start | bytes 6291464 | tf_op jit(solution)/shard_map/ppermute | solution.py:658
  55.1 38.0 %collective-permute-start.3 = (bf16[256,32]{0,1:T(8,128)(2,1)}, bf16[256,32]{0,1:T(8,128)(2,1)}, u32[]{:S(2)}, u32[]{:S(2)}) collective-permute-start(bf16[256,32]{0,1:T(8,128)(2,1)} %param.17), channel_id=1, source_target_pairs={{0,1},{1,0},{2,3},{3,2},{4,5},{5,4},{6,7},{7,6},{8,9},{9,8},{10,11... | collective-permute-start | bytes 49160 | tf_op jit(solution)/shard_map/ppermute | solution.py:643
  59.6 107.0 %collective-permute-start.8 = (bf16[256,4096]{1,0:T(8,128)(2,1)}, bf16[256,4096]{1,0:T(8,128)(2,1)}, u32[]{:S(2)}, u32[]{:S(2)}) collective-permute-start(bf16[256,4096]{1,0:T(8,128)(2,1)} %pick_channels.6), channel_id=1, source_target_pairs={{0,1},{1,0},{2,3},{3,2},{4,5},{5,4},{6,7},{7,6},{8,9},{9,8},{10,11... | collective-permute-start | bytes 6291464 | tf_op jit(solution)/shard_map/ppermute | solution.py:639
  64.6 4.2 copy-start.26
  64.6 7.6 %copy-start.4 = (bf16[256,512]{1,0:T(8,128)(2,1)S(1)}, bf16[256,512]{1,0:T(8,128)(2,1)}, u32[]{:S(2)}) copy-start(bf16[256,512]{1,0:T(8,128)(2,1)} %low_own_ref.3) | copy-start | bytes 786436
  64.6 102.0 %collective-permute-start.9 = (bf16[256,4096]{1,0:T(8,128)(2,1)}, bf16[256,4096]{1,0:T(8,128)(2,1)}, u32[]{:S(2)}, u32[]{:S(2)}) collective-permute-start(bf16[256,4096]{1,0:T(8,128)(2,1)} %pick_channels.7), channel_id=1, source_target_pairs={{0,1},{1,0},{2,3},{3,2},{4,5},{5,4},{6,7},{7,6},{8,9},{9,8},{10,11... | collective-permute-start | bytes 6291464 | tf_op jit(solution)/shard_map/ppermute | solution.py:639
  71.0 0.6 copy-start.24
  75.2 17.8 %copy-start.19 = (bf16[4,2048]{1,0:T(4,128)(2,1)S(1)}, bf16[4,2048]{1,0:T(4,128)(2,1)}, u32[]{:S(2)}) copy-start(bf16[4,2048]{1,0:T(4,128)(2,1)} %param.18) | copy-start | bytes 49156
  85.4 5.1 copy-start.25
  85.4 5.7 copy-start.23
  85.4 7.6 %copy-start.17 = (f32[16,2048]{1,0:T(8,128)S(1)}, f32[16,2048]{1,0:T(8,128)}, u32[]{:S(2)}) copy-start(f32[16,2048]{1,0:T(8,128)} %param.22) | copy-start | bytes 393220
  85.5 7.6 %copy-start.20 = (f32[2048]{0:T(1024)S(1)}, f32[2048]{0:T(1024)}, u32[]{:S(2)}) copy-start(f32[2048]{0:T(1024)} %param.19) | copy-start | bytes 24580
  85.5 7.6 %copy-start.21 = (f32[2048]{0:T(1024)S(1)}, f32[2048]{0:T(1024)}, u32[]{:S(2)}) copy-start(f32[2048]{0:T(1024)} %param.21) | copy-start | bytes 24580
  85.5 7.6 %copy-start.22 = (f32[2048]{0:T(1024)S(1)}, f32[2048]{0:T(1024)}, u32[]{:S(2)}) copy-start(f32[2048]{0:T(1024)} %param.23) | copy-start | bytes 24580
  86.3 78.0 %all-to-all-start.1 = ((bf16[256,8,256]{0,2,1:T(8,128)(2,1)}), bf16[256,8,256]{0,2,1:T(8,128)(2,1)}, u32[]{:S(2)}, u32[]{:S(2)}) async-start(bf16[256,8,256]{0,2,1:T(8,128)(2,1)} %bitcast.11), calls=%async_computation.1 | async-start | bytes 2097152 | tf_op jit(solution)/shard_map/all_to_all | solution.py:621
  93.1 67.4 %copy-start.13 = (f32[24,2048]{1,0:T(8,128)}, f32[24,2048]{1,0:T(8,128)S(1)}, u32[]{:S(2)}) copy-start(f32[24,2048]{1,0:T(8,128)S(1)} %concatenate.24) | copy-start | bytes 589828
  93.2 40.1 %collective-permute-start.6 = (f32[24,2048]{1,0:T(8,128)S(1)}, f32[24,2048]{1,0:T(8,128)S(1)}, u32[]{:S(2)}, u32[]{:S(2)}) collective-permute-start(f32[24,2048]{1,0:T(8,128)S(1)} %concatenate.24), channel_id=1, source_target_pairs={{0,6},{2,0},{4,2},{6,4},{1,7},{3,1},{5,3},{7,5},{8,14},{10,8},{12,... | collective-permute-start | bytes 589832 | tf_op jit(solution)/shard_map/ppermute | solution.py:662
  133.3 27.3 %copy-start.15 = (f32[24,2048]{1,0:T(8,128)}, f32[24,2048]{1,0:T(8,128)S(1)}, u32[]{:S(2)}) copy-start(f32[24,2048]{1,0:T(8,128)S(1)} %collective-permute-done.6) | copy-start | bytes 589828
  133.3 19.0 %collective-permute-start.5 = (f32[24,2048]{1,0:T(8,128)S(1)}, f32[24,2048]{1,0:T(8,128)S(1)}, u32[]{:S(2)}, u32[]{:S(2)}) collective-permute-start(f32[24,2048]{1,0:T(8,128)S(1)} %concatenate.24), channel_id=1, source_target_pairs={{0,4},{2,6},{4,0},{6,2},{1,5},{3,7},{5,1},{7,3},{8,12},{10,14},{12... | collective-permute-start | bytes 589832 | tf_op jit(solution)/shard_map/ppermute | solution.py:662
  152.3 8.3 %copy-start.16 = (f32[24,2048]{1,0:T(8,128)}, f32[24,2048]{1,0:T(8,128)S(1)}, u32[]{:S(2)}) copy-start(f32[24,2048]{1,0:T(8,128)S(1)} %collective-permute-done.5) | copy-start | bytes 589828
  152.3 8.2 %collective-permute-start.4 = (f32[24,2048]{1,0:T(8,128)S(1)}, f32[24,2048]{1,0:T(8,128)S(1)}, u32[]{:S(2)}, u32[]{:S(2)}) collective-permute-start(f32[24,2048]{1,0:T(8,128)S(1)} %concatenate.24), channel_id=1, source_target_pairs={{0,2},{2,4},{4,6},{6,0},{1,3},{3,5},{5,7},{7,1},{8,10},{10,12},{12... | collective-permute-start | bytes 589832 | tf_op jit(solution)/shard_map/ppermute | solution.py:662
  160.5 1.9 collective-permute-start.7
  161.7 8.4 %copy-start = (f32[4,24,2048]{2,1,0:T(8,128)}, f32[4,24,2048]{2,1,0:T(8,128)S(1)}, u32[]{:S(2)}) copy-start(f32[4,24,2048]{2,1,0:T(8,128)S(1)} %pad_maximum_fusion.2.param_ref.refs_3_.refs_4_) | copy-start | bytes 2359300
  162.4 7.7 %copy-start.5 = (bf16[256,512]{1,0:T(8,128)(2,1)}, bf16[256,512]{1,0:T(8,128)(2,1)S(1)}, u32[]{:S(2)}) copy-start(bf16[256,512]{1,0:T(8,128)(2,1)S(1)} %collective-permute-done.7.low_other_ref) | copy-start | bytes 786436
  166.6 3.6 copy-start.1
  166.6 3.6 copy-start.6
  171.7 3.8 copy-start.3
  171.7 31.1 %copy-start.12 = (bf16[512,16,16]{0,2,1:T(8,128)(2,1)S(1)}, bf16[512,16,16]{0,2,1:T(8,128)(2,1)}, u32[]{:S(2)}) copy-start(bf16[512,16,16]{0,2,1:T(8,128)(2,1)} %broadcast_select_fusion) | copy-start | bytes 786436
  171.7 116.9 %all-to-all-start.2 = ((bf16[256,8,512]{2,0,1:T(8,128)(2,1)}), bf16[256,8,512]{2,0,1:T(8,128)(2,1)S(1)}, u32[]{:S(2)}, u32[]{:S(2)}) async-start(bf16[256,8,512]{2,0,1:T(8,128)(2,1)} %bitcast.58), calls=%async_computation.2 | async-start | bytes 4194304 | tf_op jit(solution)/shard_map/all_to_all | solution.py:706
  175.4 26.1 %collective-permute-start.13 = (bf16[4,128,1024]{2,1,0:T(8,128)(2,1)S(1)}, bf16[4,128,1024]{2,1,0:T(8,128)(2,1)S(1)}, u32[]{:S(2)}, u32[]{:S(2)}) collective-permute-start(bf16[4,128,1024]{2,1,0:T(8,128)(2,1)S(1)} %copy-done.3), channel_id=1, source_target_pairs={{0,8},{8,0},{16,24},{24,16},{1,9},{9,1},{17,25},{25,17},{2,10},{10... | collective-permute-start | bytes 3145736 | tf_op jit(solution)/shard_map/ppermute | solution.py:618
  175.5 48.7 %collective-permute-start.14 = (bf16[4,128,1024]{2,1,0:T(8,128)(2,1)S(1)}, bf16[4,128,1024]{2,1,0:T(8,128)(2,1)}, u32[]{:S(2)}, u32[]{:S(2)}) collective-permute-start(bf16[4,128,1024]{2,1,0:T(8,128)(2,1)S(1)} %copy-done.3), channel_id=1, source_target_pairs={{0,16},{8,24},{16,0},{24,8},{1,17},{9,25},{17,1},{25,9},{2,18},{10... | collective-permute-start | bytes 3145736 | tf_op jit(solution)/shard_map/ppermute | solution.py:618
  176.3 47.9 %collective-permute-start.15 = (bf16[4,128,1024]{2,1,0:T(8,128)(2,1)S(1)}, bf16[4,128,1024]{2,1,0:T(8,128)(2,1)}, u32[]{:S(2)}, u32[]{:S(2)}) collective-permute-start(bf16[4,128,1024]{2,1,0:T(8,128)(2,1)S(1)} %copy-done.3), channel_id=1, source_target_pairs={{0,24},{8,16},{16,8},{24,0},{1,25},{9,17},{17,9},{25,1},{2,26},{10... | collective-permute-start | bytes 3145736 | tf_op jit(solution)/shard_map/ppermute | solution.py:618
  179.0 109.5 %collective-permute-start.16 = (bf16[2048,256]{1,0:T(8,128)(2,1)}, bf16[2048,256]{1,0:T(8,128)(2,1)}, u32[]{:S(2)}, u32[]{:S(2)}) collective-permute-start(bf16[2048,256]{1,0:T(8,128)(2,1)} %bitcast.59), channel_id=1, source_target_pairs={{0,8},{8,0},{16,24},{24,16},{1,9},{9,1},{17,25},{25,17},{2,10},{10... | collective-permute-start | bytes 3145736 | tf_op jit(solution)/shard_map/ppermute | solution.py:707
  179.1 109.5 %collective-permute-start.17 = (bf16[2048,256]{1,0:T(8,128)(2,1)}, bf16[2048,256]{1,0:T(8,128)(2,1)}, u32[]{:S(2)}, u32[]{:S(2)}) collective-permute-start(bf16[2048,256]{1,0:T(8,128)(2,1)} %bitcast.60), channel_id=1, source_target_pairs={{0,16},{8,24},{16,0},{24,8},{1,17},{9,25},{17,1},{25,9},{2,18},{10... | collective-permute-start | bytes 3145736 | tf_op jit(solution)/shard_map/ppermute | solution.py:707
  201.5 1.0 copy-start.8
  202.5 86.0 %collective-permute-start.18 = (bf16[2048,256]{1,0:T(8,128)(2,1)}, bf16[2048,256]{1,0:T(8,128)(2,1)}, u32[]{:S(2)}, u32[]{:S(2)}) collective-permute-start(bf16[2048,256]{1,0:T(8,128)(2,1)} %bitcast.61), channel_id=1, source_target_pairs={{0,24},{8,16},{16,8},{24,0},{1,25},{9,17},{17,9},{25,1},{2,26},{10... | collective-permute-start | bytes 3145736 | tf_op jit(solution)/shard_map/ppermute | solution.py:707
  288.6 41.3 %copy-start.2 = (bf16[256,8,512]{2,0,1:T(8,128)(2,1)}, bf16[256,8,512]{2,0,1:T(8,128)(2,1)S(1)}, u32[]{:S(2)}) copy-start(bf16[256,8,512]{2,0,1:T(8,128)(2,1)S(1)} %all-to-all-done.2) | copy-start | bytes 6291460
  288.6 41.3 %all-to-all-start.3 = ((bf16[16,32,256]{2,1,0:T(8,128)(2,1)}), bf16[16,32,256]{2,1,0:T(8,128)(2,1)S(1)}, u32[]{:S(2)}, u32[]{:S(2)}) async-start(bf16[16,32,256]{2,1,0:T(8,128)(2,1)} %get-tuple-element.81), calls=%async_computation.3 | async-start | bytes 524288 | tf_op jit(solution)/shard_map/all_to_all | solution.py:685
  329.9 0.7 copy-start.11
  333.1 43.5 %all-to-all-start.4 = ((bf16[16,16,256]{2,1,0:T(8,128)(2,1)}), bf16[16,16,256]{2,1,0:T(8,128)(2,1)S(1)}, u32[]{:S(2)}, u32[]{:S(2)}) async-start(bf16[16,16,256]{2,1,0:T(8,128)(2,1)} %state_combine.2), calls=%async_computation.4 | async-start | bytes 262144 | tf_op jit(solution)/shard_map/all_to_all | solution.py:685
  340.0 35.0 %copy-start.18 = (bf16[8,32,256]{2,1,0:T(8,128)(2,1)S(1)}, bf16[8,32,256]{2,1,0:T(8,128)(2,1)}, u32[]{:S(2)}) copy-start(bf16[8,32,256]{2,1,0:T(8,128)(2,1)} %get-tuple-element.86) | copy-start | bytes 393220
  376.6 65.2 %copy-start.14 = (bf16[16,16,256]{2,1,0:T(8,128)(2,1)}, bf16[16,16,256]{2,1,0:T(8,128)(2,1)S(1)}, u32[]{:S(2)}) copy-start(bf16[16,16,256]{2,1,0:T(8,128)(2,1)S(1)} %all-to-all-done.4.refs_2_) | copy-start | bytes 393220
  376.6 65.2 %all-to-all-start.5 = ((bf16[16,32,256]{2,1,0:T(8,128)(2,1)}), bf16[16,32,256]{2,1,0:T(8,128)(2,1)S(1)}, u32[]{:S(2)}, u32[]{:S(2)}) async-start(bf16[16,32,256]{2,1,0:T(8,128)(2,1)} %pad_maximum_fusion.5), calls=%async_computation.5 | async-start | bytes 524288 | tf_op jit(solution)/shard_map/all_to_all | solution.py:685
  441.8 0.7 copy-start.10
  445.1 48.7 %all-to-all-start.6 = ((bf16[16,16,256]{2,1,0:T(8,128)(2,1)}), bf16[16,16,256]{2,1,0:T(8,128)(2,1)S(1)}, u32[]{:S(2)}, u32[]{:S(2)}) async-start(bf16[16,16,256]{2,1,0:T(8,128)(2,1)} %state_combine.3), calls=%async_computation.6 | async-start | bytes 262144 | tf_op jit(solution)/shard_map/all_to_all | solution.py:685
  493.8 0.7 copy-start.7
  494.4 63.5 %all-to-all-start.7 = ((bf16[8,256,512]{2,1,0:T(8,128)(2,1)}), bf16[8,256,512]{2,1,0:T(8,128)(2,1)S(1)}, u32[]{:S(2)}, u32[]{:S(2)}) async-start(bf16[8,256,512]{2,1,0:T(8,128)(2,1)} %bitcast.33), calls=%async_computation.7 | async-start | bytes 4194304 | tf_op jit(solution)/shard_map/all_to_all | solution.py:727
  499.4 47.6 %collective-permute-start.19 = (bf16[256,4096]{1,0:T(8,128)(2,1)}, bf16[256,4096]{1,0:T(8,128)(2,1)}, u32[]{:S(2)}, u32[]{:S(2)}) collective-permute-start(bf16[256,4096]{1,0:T(8,128)(2,1)} %get-tuple-element.118), channel_id=1, source_target_pairs={{0,1},{1,0},{2,3},{3,2},{4,5},{5,4},{6,7},{7,6},{8,9},{9,8},{10,11... | collective-permute-start | bytes 6291464 | tf_op jit(solution)/shard_map/ppermute | solution.py:726
  523.2 28.3 %collective-permute-start.20 = (bf16[256,2048]{1,0:T(8,128)(2,1)}, bf16[256,2048]{1,0:T(8,128)(2,1)S(1)}, u32[]{:S(2)}, u32[]{:S(2)}) collective-permute-start(bf16[256,2048]{1,0:T(8,128)(2,1)} %get-tuple-element.119), channel_id=1, source_target_pairs={{0,1},{1,0},{2,3},{3,2},{4,5},{5,4},{6,7},{7,6},{8,9},{9,8},{10,11... | collective-permute-start | bytes 3145736 | tf_op jit(solution)/shard_map/ppermute | solution.py:729
  546.5 8.6 %collective-permute-start.21 = (bf16[256,2048]{1,0:T(8,128)(2,1)}, bf16[256,2048]{1,0:T(8,128)(2,1)}, u32[]{:S(2)}, u32[]{:S(2)}) collective-permute-start(bf16[256,2048]{1,0:T(8,128)(2,1)} %get-tuple-element.120), channel_id=1, source_target_pairs={{0,1},{1,0},{2,3},{3,2},{4,5},{5,4},{6,7},{7,6},{8,9},{9,8},{10,11... | collective-permute-start | bytes 3145736 | tf_op jit(solution)/shard_map/ppermute | solution.py:731
  551.5 1.0 copy-start.9
Sparse Core Ops, SparseCore 0:
  37.7 103.3 all-gather.2

commit v3 on v2

--- a/solution.py
+++ b/solution.py
@@ -662,7 +662,6 @@
     params = jnp.stack([packed] + [lax.ppermute(packed, "chip", move) for move in far_moves])
 
     share = cols // chunks
-    split = chip_count // 2
 
     def scan_part(piece, x_piece, lows, weights, first, blocks):
         return run_scan(
@@ -694,44 +693,33 @@
     lows_first = (by_flip(delta_low), by_flip(low_other))
     lows_later = (delta_low, low_other)
     tables = flash_tables(span_order, my_blocks, blk)
-    (
-        queries, kv_local, gate_other, inject, read, params, my_rates, tables, order, lows_first,
-        x_other,
-    ) = lax.optimization_barrier(
-        (
-            queries, kv_local, gate_other, inject, read, params, my_rates, tables, order,
-            lows_first, x_other,
+    gate_other, inject, read, params, my_rates, tables, order, lows_first, x_other = (
+        lax.optimization_barrier(
+            (gate_other, inject, read, params, my_rates, tables, order, lows_first, x_other)
         )
+    )
+    made_0 = scan_part(0, x_other[0], lows_first, weights_first, 0, chip_count)
+    x_now, sent_0, queries, kv_local = lax.optimization_barrier(
+        (x_other[1], made_0[2], queries, kv_local)
     )
     q_local = lax.all_to_all(queries, ulys, split_axis=1, concat_axis=0, tiled=True)
     kv_parts = [kv_local] + [lax.ppermute(kv_local, "blk", move) for move in flips]
-    made_0 = scan_part(0, x_other[0], lows_first, weights_first, 0, chip_count)
-    x_now, sent_0, q_local, kv_parts, my_rates = lax.optimization_barrier(
-        (x_other[1], made_0[2], q_local, kv_parts, my_rates)
-    )
-    got_0 = to_owners(sent_0)
-    made_1a = scan_part(1, x_now, lows_later, weights_later, 0, split)
-    x_now, got_0, sent_1a = lax.optimization_barrier((x_now, got_0, made_1a[2]))
-    enter_0 = to_owners(run_combine(order, got_0, my_rates[0]))
-    made_1b = scan_part(1, x_now, lows_later, weights_later, split, chip_count - split)
-    enter_0, sent_1, q_local = lax.optimization_barrier(
-        (enter_0, jnp.concatenate([sent_1a, made_1b[2]], axis=0), q_local)
-    )
-    got_1 = to_owners(sent_1)
+    made_1 = scan_part(1, x_now, lows_later, weights_later, 0, chip_count)
+    sent, q_local = lax.optimization_barrier(
+        (jnp.concatenate([sent_0, made_1[2]], axis=2), q_local)
+    )
+    got = to_owners(sent)
     attended = run_flash(tables, q_local, kv_parts)
-    enter_0, got_1, attended = lax.optimization_barrier((enter_0, got_1, attended))
-    enter_1 = to_owners(run_combine(order, got_1, my_rates[1]))
-    full, theirs_0 = correct_part(None, made_0, enter_0, 0, 0, 0, chip_count)
-    full, enter_1, attended = lax.optimization_barrier((full, enter_1, attended))
+    got, attended = lax.optimization_barrier((got, attended))
+    enter = to_owners(run_combine(order, got, jnp.concatenate(my_rates, axis=1)))
+    enter, attended = lax.optimization_barrier((enter, attended))
+    attention_output = lax.all_to_all(attended, ulys, split_axis=0, concat_axis=1, tiled=True)
+    full, theirs_0 = correct_part(None, made_0, enter[:, :, :share], 0, 0, 0, chip_count)
     back_0 = lax.ppermute(theirs_0, "core", swap)
-    attention_output = lax.all_to_all(attended, ulys, split_axis=0, concat_axis=1, tiled=True)
-    full, theirs_1a = correct_part(full, made_1a, enter_1, 1, 0, 0, split)
-    back_1a = lax.ppermute(theirs_1a, "core", swap)
-    full, theirs_1b = correct_part(full, made_1b, enter_1, 1, split, 0, chip_count - split)
-    back_1b = lax.ppermute(theirs_1b, "core", swap)
+    full, theirs_1 = correct_part(full, made_1, enter[:, :, share:], 1, 0, 0, chip_count)
+    back_1 = lax.ppermute(theirs_1, "core", swap)
     full = run_place(core_arr, full, back_0, 0, width, 0)
-    full = run_place(core_arr, full, back_1a, 1, width, 0)
-    mamba_output = run_place(core_arr, full, back_1b, 1, width, split)
+    mamba_output = run_place(core_arr, full, back_1, 1, width, 0)
     return (mamba_output, attention_output)
 
 

time: 568 us -> 539 us (0.949)
  starting transfers between devices: 73.5 us -> 51.8 us
  blocking collectives: 0 us -> 16.3 us
  Pallas kernels: 314 us -> 300 us
  waiting for transfers between devices: 120 us -> 113 us
    all_to_all x4 -> x1, starting transfers between devices: 27.2 us -> 6.36 us  [to_owners(): return lax.all_to_all(array, chips, split_axis=0, concat_axis=0, tiled=True)]
    all_to_all x0 -> x1, blocking collectives: none -> 16.3 us  [to_owners(): return lax.all_to_all(array, chips, split_axis=0, concat_axis=0, tiled=True)]
    ppermute x3, starting transfers between devices: 14.4 us -> 4.78 us  [local(): lax.ppermute(packed, 'chip', move)]
    ppermute x3, waiting for transfers between devices: 42.3 us -> 32.9 us  [local(): lax.ppermute(shards_first, 'blk', move)]
    ppermute x3, waiting for transfers between devices: 49.9 us -> 59 us  [local(): lax.ppermute(packed, 'chip', move)]
    ppermute x3, waiting for transfers between devices: 19.8 us -> 11.4 us  [local(): lax.ppermute(part_first, 'chip', move)]
    unnamed x56 -> x38, local copies, waits for them, and re-layouts: 8.29 us -> 1.52 us
    all_to_all x1, starting transfers between devices: 6.06 us -> 12.7 us  [local(): lax.all_to_all(jnp.broadcast_to(tail[None], (chunks, CONV - 1, PIECES * c...]
  transfers between devices with their start and end apart: 31 -> 27, of which waited for: 8 -> 7; matrix products, arithmetic and copies ran while one was open for 6% -> 7% of each run, Pallas kernels for 54% -> 55%
where the time goes in v3:
time: 539 us; the launch traced here: 537 us
  Pallas kernels  300 us (56%)
  waiting for transfers between devices  113 us (21%)
  starting transfers between devices  51.8 us (10%)
  local copies, waits for them, and re-layouts  24.3 us (5%)
  blocking collectives  16.3 us (3%)
  between operations  15.6 us (3%)
  other arithmetic  15 us (3%)
    pallas_call x2, Pallas kernels, run_scan(): pl.pallas_call(functools.partial(scan_kernel, sources=sources), grid_spec...  129 us
    pallas_call x2, Pallas kernels, run_correct(): pl.pallas_call(functools.partial(correct_kernel, resumed=resumed), grid_s...  83.6 us
    ppermute x3, waiting for transfers between devices, local(): lax.ppermute(packed, 'chip', move)  59 us
    pallas_call x1, Pallas kernels, run_flash(): pl.pallas_call(functools.partial(flash_kernel, heads=heads, rows=rows, so...  58.2 us
    ppermute x3, waiting for transfers between devices, local(): lax.ppermute(shards_first, 'blk', move)  32.9 us
    pallas_call x4, Pallas kernels, run_pick(): pl.pallas_call(copy_kernel, grid_spec=pltpu.PrefetchScalarGridSpec(num_sc...  18 us
    all_to_all x1, blocking collectives, to_owners(): return lax.all_to_all(array, chips, split_axis=0, concat_axis=0, tiled=True)  16.3 us
    all_to_all x1, starting transfers between devices, local(): lax.all_to_all(jnp.broadcast_to(tail[None], (chunks, CONV - 1, PIECES * c...  12.7 us
  transfers between devices with their start and end apart: 27, of which 7 were waited for; matrix products, arithmetic and copies ran while one was open for 7% of the time, Pallas kernels for 55%

profile of v3, /device:TPU:0, one launch (start us, length us, event | category | flops | bytes accessed | tf_op | source)
XLA Modules:
  0.0 537.3 jit_solution(1165130315005689239)
XLA Ops:
  7.2 1.8 fusion.12
  9.0 3.1 collective-permute-start.10
  12.0 2.6 collective-permute-start.11
  14.6 1.3 collective-permute-start.12
  16.0 3.0 concatenate.26
  19.0 0.7 collective-permute-start.3
  19.7 1.0 slice.32
  21.4 11.2 %collective-permute-done.11 = bf16[128,1024]{1,0:T(8,128)(2,1)S(1)} collective-permute-done((bf16[128,1024]{1,0:T(8,128)(2,1)S(1)}, bf16[128,1024]{1,0:T(8,128)(2,1)S(1)}, u32[]{:S(2)}, u32[]{:S(2)}) %collective-permute-start.11) | collective-permute-done | bytes 262176 | tf_op jit(solution)/shard_map/ppermute | solution.py:559
  32.8 1.4 broadcast_in_dim.143
  34.2 12.7 %all-to-all-start = ((bf16[16,3,8192]{2,1,0:T(4,128)(2,1)}), bf16[16,3,8192]{2,1,0:T(4,128)(2,1)S(1)}, u32[]{:S(2)}, u32[]{:S(2)}) async-start(bf16[16,3,8192]{2,1,0:T(4,128)(2,1)} %broadcast_in_dim.143), calls=%async_computation | async-start | bytes 2097152 | tf_op jit(solution)/shard_map/all_to_all | solution.py:595
  46.9 0.7 pad_add_fusion.core_ref
  47.6 4.5 pick_channels.4
  52.1 4.5 pick_channels.5
  57.2 4.5 pick_channels.6
  62.2 0.6 fusion.15
  63.7 1.2 copy.36
  65.1 0.7 fusion.8
  65.8 0.6 select_reduce_fusion.order_ref
  66.5 1.1 pad_maximum_fusion
  67.6 1.8 compare_convert_fusion
  69.3 4.5 pick_channels.7
  74.7 9.8 %all-to-all-done = bf16[16,3,8192]{2,1,0:T(4,128)(2,1)S(1)} async-done(((bf16[16,3,8192]{2,1,0:T(4,128)(2,1)}), bf16[16,3,8192]{2,1,0:T(4,128)(2,1)S(1)}, u32[]{:S(2)}, u32[]{:S(2)}) %all-to-all-start) | async-done | bytes 786464 | tf_op jit(solution)/shard_map/all_to_all | solution.py:595
  84.5 0.9 fusion
  85.5 0.7 concatenate.29.halo_ref
  86.2 3.6 all-to-all-start.1
  89.8 2.8 collective-permute-start.4
  92.6 0.6 iota_compare_fusion
  93.2 54.1 %collective-permute-done.4 = f32[24,2048]{1,0:T(8,128)S(1)} collective-permute-done((f32[24,2048]{1,0:T(8,128)}, f32[24,2048]{1,0:T(8,128)S(1)}, u32[]{:S(2)}, u32[]{:S(2)}) %collective-permute-start.4) | collective-permute-done | bytes 196640 | tf_op jit(solution)/shard_map/ppermute | solution.py:662
  147.3 1.3 collective-permute-start.5
  149.1 4.8 collective-permute-done.5
  154.5 0.7 constant_dynamic-slice_fusion.9
  155.2 0.8 maximum_select_fusion
  156.1 1.0 collective-permute-start.14
  157.1 2.5 collective-permute-start.15
  159.6 0.6 fusion.14
  160.2 1.6 copy.34
  161.8 1.7 reshape.117
  163.5 1.5 broadcast_select_fusion
  165.0 1.3 pad_maximum_fusion.2.param_ref.refs_3_.refs_4_
  166.2 0.7 multiply_bitcast_fusion
  167.0 0.9 pad_maximum_fusion.4
  167.9 2.6 broadcast_in_dim.125.inject_ref
  170.6 0.8 copy.39.read_ref.refs_4_.refs_5_
  171.4 10.7 %collective-permute-done.13.refs_1_ = bf16[4,128,1024]{2,1,0:T(8,128)(2,1)S(1)} collective-permute-done((bf16[4,128,1024]{2,1,0:T(8,128)(2,1)S(1)}, bf16[4,128,1024]{2,1,0:T(8,128)(2,1)S(1)}, u32[]{:S(2)}, u32[]{:S(2)}) %collective-permute-start.13) | collective-permute-done | bytes 1048608 | tf_op jit(solution)/shard_map/ppermute | solution.py:618
  182.1 22.2 %collective-permute-done.14.refs_2_ = bf16[4,128,1024]{2,1,0:T(8,128)(2,1)} collective-permute-done((bf16[4,128,1024]{2,1,0:T(8,128)(2,1)S(1)}, bf16[4,128,1024]{2,1,0:T(8,128)(2,1)}, u32[]{:S(2)}, u32[]{:S(2)}) %collective-permute-start.14) | collective-permute-done | bytes 1048608 | tf_op jit(solution)/shard_map/ppermute | solution.py:618
  204.3 64.3 %token_scan.2 = (f32[32,512,128]{2,1,0:T(8,128)}, bf16[512,4096]{1,0:T(8,128)(2,1)}, bf16[16,32,256]{2,1,0:T(8,128)(2,1)}) custom-call(s32[2]{0:T(128)} %pad_add_fusion.core_ref, bf16[256,16384]{1,0:T(8,128)(2,1)} %own_ref.3, bf16[256,4096]{1,0:T(8,128)(2,1)} %collective-permute-done.7.other_ref, bf16[8,8192]{1,0:T(8,128)(2,1)} %concatenate.29.halo_ref, ...), custom_call_target="tpu_custom_call" | custom-call | tf_op jit(solution)/shard_map/token_scan/pallas_call | solution.py:370
  269.2 3.5 copy.56
  272.7 4.9 all-to-all-start.2
  277.6 1.6 collective-permute-start.16
  279.6 1.5 collective-permute-start.18
  281.1 64.3 %token_scan.3 = (f32[32,512,128]{2,1,0:T(8,128)}, bf16[512,4096]{1,0:T(8,128)(2,1)}, bf16[16,32,256]{2,1,0:T(8,128)(2,1)}) custom-call(s32[2]{0:T(128)} %pad_add_fusion.core_ref, bf16[256,16384]{1,0:T(8,128)(2,1)} %own_ref.3, bf16[256,4096]{1,0:T(8,128)(2,1)} %collective-permute-done.8.other_ref, bf16[8,8192]{1,0:T(8,128)(2,1)} %concatenate.29.halo_ref, ...), custom_call_target="tpu_custom_call" | custom-call | tf_op jit(solution)/shard_map/token_scan/pallas_call | solution.py:370
  345.4 1.8 pad_maximum_fusion.3
  347.2 6.4 %all-to-all-start.3 = ((bf16[16,32,512]{2,1,0:T(8,128)(2,1)}), bf16[16,32,512]{2,1,0:T(8,128)(2,1)}, u32[]{:S(2)}, u32[]{:S(2)}) async-start(bf16[16,32,512]{2,1,0:T(8,128)(2,1)} %pad_maximum_fusion.3), calls=%async_computation.3 | async-start | bytes 1048576 | tf_op jit(solution)/shard_map/all_to_all | solution.py:684
  353.6 0.6 pad_maximum_fusion.6.rate_ref
  354.2 58.2 %causal_attention.1 = bf16[2048,512]{1,0:T(8,128)(2,1)} custom-call(s32[9]{0:T(128)} %compare_convert_fusion.2.side_ref, s32[9]{0:T(128)} %get-tuple-element.65.flip_ref, s32[9]{0:T(128)} %get-tuple-element.66.half_ref, s32[9]{0:T(128)} %get-tuple-element.69.diag_ref.last_ref, s32[9]{0:T(128)} %get-tuple-element.68.first_ref, ...), custom_call_target="tpu_custom_call" | custom-call | tf_op jit(solution)/shard_map/causal_attention/pallas_call | solution.py:489
  412.4 2.7 state_combine.1
  415.2 16.3 %all_to_all.72 = bf16[16,16,512]{2,1,0:T(8,128)(2,1)S(1)} all-to-all(bf16[16,16,512]{2,1,0:T(8,128)(2,1)} %state_combine.1), channel_id=1, replica_groups=mesh['blk'=4,'chip'=4,'core'=2] {'blk','chip'}, dimensions={0} | all-to-all | bytes 524288 | tf_op jit(solution)/shard_map/all_to_all | solution.py:684
  431.5 3.6 all-to-all-start.5
  435.1 0.7 fusion.13
  435.8 41.8 %state_correction.2 = (bf16[256,16384]{1,0:T(8,128)(2,1)}, bf16[256,4096]{1,0:T(8,128)(2,1)}) custom-call(s32[2]{0:T(128)} %pad_add_fusion.core_ref, f32[32,512,128]{2,1,0:T(8,128)} %get-tuple-element.52.refs_0_, bf16[512,4096]{1,0:T(8,128)(2,1)} %get-tuple-element.53.refs_1_, bf16[16,16,256]{2,1,0:T(8,128)(2,1)} %get-tuple-element.93.refs_2_, ...), custom_call_target="tpu_custom_call" | custom-call | tf_op jit(solution)/shard_map/state_correction/pallas_call | solution.py:422
  478.0 41.8 %state_correction.3 = (bf16[256,16384]{1,0:T(8,128)(2,1)}, bf16[256,4096]{1,0:T(8,128)(2,1)}) custom-call(s32[2]{0:T(128)} %pad_add_fusion.core_ref, bf16[256,16384]{1,0:T(8,128)(2,1)} %get-tuple-element.78.refs_0_, f32[32,512,128]{2,1,0:T(8,128)} %get-tuple-element.79.refs_1_, ...), custom_call_target="tpu_custom_call", output_to_operand_aliasing={{0}: (1, {})} | custom-call | tf_op jit(solution)/shard_map/state_correction/pallas_call | solution.py:422
  519.9 4.5 place_channels.2.buffer_ref
  524.4 4.5 place_channels.3
  528.8 1.6 copy.49
  (92 shorter events, 5.5 us)
Async XLA Ops:
  7.2 273.9 %all-gather.3.cloned.1.call-start = ((), (), s32[]{:S(2)}) async-start(), calls=%async_computation.6 | async-start | bytes 4456448 | tf_op jit(solution)/shard_map/all_gather | solution.py:616
  9.0 12.4 %collective-permute-start.10 = (bf16[128,1024]{1,0:T(8,128)(2,1)S(1)}, bf16[128,1024]{1,0:T(8,128)(2,1)S(1)}, u32[]{:S(2)}, u32[]{:S(2)}) collective-permute-start(bf16[128,1024]{1,0:T(8,128)(2,1)S(1)} %get-tuple-element.89), channel_id=1, source_target_pairs={{0,2},{2,4},{4,6},{6,0},{1,3},{3,5},{5,7},{7,1},{8,10},{10,12},{12... | collective-permute-start | bytes 786440 | tf_op jit(solution)/shard_map/ppermute | solution.py:559
  12.0 20.6 %collective-permute-start.11 = (bf16[128,1024]{1,0:T(8,128)(2,1)S(1)}, bf16[128,1024]{1,0:T(8,128)(2,1)S(1)}, u32[]{:S(2)}, u32[]{:S(2)}) collective-permute-start(bf16[128,1024]{1,0:T(8,128)(2,1)S(1)} %get-tuple-element.89), channel_id=1, source_target_pairs={{0,4},{2,6},{4,0},{6,2},{1,5},{3,7},{5,1},{7,3},{8,12},{10,14},{12... | collective-permute-start | bytes 786440 | tf_op jit(solution)/shard_map/ppermute | solution.py:559
  14.6 18.0 %collective-permute-start.12 = (bf16[128,1024]{1,0:T(8,128)(2,1)S(1)}, bf16[128,1024]{1,0:T(8,128)(2,1)S(1)}, u32[]{:S(2)}, u32[]{:S(2)}) collective-permute-start(bf16[128,1024]{1,0:T(8,128)(2,1)S(1)} %get-tuple-element.89), channel_id=1, source_target_pairs={{0,6},{2,0},{4,2},{6,4},{1,7},{3,1},{5,3},{7,5},{8,14},{10,8},{12,... | collective-permute-start | bytes 786440 | tf_op jit(solution)/shard_map/ppermute | solution.py:559
  19.0 70.8 %collective-permute-start.3 = (f32[24,2048]{1,0:T(8,128)}, f32[24,2048]{1,0:T(8,128)}, u32[]{:S(2)}, u32[]{:S(2)}) collective-permute-start(f32[24,2048]{1,0:T(8,128)} %concatenate.26), channel_id=1, source_target_pairs={{0,2},{2,4},{4,6},{6,0},{1,3},{3,5},{5,7},{7,1},{8,10},{10,12},{12... | collective-permute-start | bytes 589832 | tf_op jit(solution)/shard_map/ppermute | solution.py:662
  21.0 11.8 %collective-permute-start.9 = (bf16[3,8192]{1,0:T(4,128)(2,1)S(1)}, bf16[3,8192]{1,0:T(4,128)(2,1)S(1)}, u32[]{:S(2)}, u32[]{:S(2)}) collective-permute-start(bf16[3,8192]{1,0:T(4,128)(2,1)S(1)} %reshape.115), channel_id=1, source_target_pairs={{0,1},{1,0},{2,3},{3,2},{4,5},{5,4},{6,7},{7,6},{8,9},{9,8},{10,11... | collective-permute-start | bytes 147464 | tf_op jit(solution)/shard_map/ppermute | solution.py:593
  32.7 124.4 %copy-start.2 = (bf16[4,128,1024]{2,1,0:T(8,128)(2,1)}, bf16[4,128,1024]{2,1,0:T(8,128)(2,1)S(1)}, u32[]{:S(2)}) copy-start(bf16[4,128,1024]{2,1,0:T(8,128)(2,1)S(1)} %pad_maximum_fusion.1.refs_0_) | copy-start | bytes 3145732
  34.2 50.3 %all-to-all-start = ((bf16[16,3,8192]{2,1,0:T(4,128)(2,1)}), bf16[16,3,8192]{2,1,0:T(4,128)(2,1)S(1)}, u32[]{:S(2)}, u32[]{:S(2)}) async-start(bf16[16,3,8192]{2,1,0:T(4,128)(2,1)} %broadcast_in_dim.143), calls=%async_computation | async-start | bytes 2097152 | tf_op jit(solution)/shard_map/all_to_all | solution.py:595
  52.1 104.0 %collective-permute-start = (bf16[256,4096]{1,0:T(8,128)(2,1)}, bf16[256,4096]{1,0:T(8,128)(2,1)}, u32[]{:S(2)}, u32[]{:S(2)}) collective-permute-start(bf16[256,4096]{1,0:T(8,128)(2,1)} %pick_channels.4), channel_id=1, source_target_pairs={{0,1},{1,0},{2,3},{3,2},{4,5},{5,4},{6,7},{7,6},{8,9},{9,8},{10,11... | collective-permute-start | bytes 6291464 | tf_op jit(solution)/shard_map/ppermute | solution.py:658
  56.6 5.2 copy-start.15
  56.6 5.5 %copy-start.17 = (s32[8]{0:T(128)S(1)}, s32[8]{0:T(128)}, u32[]{:S(2)}) copy-start(s32[8]{0:T(128)} %param.27) | copy-start | bytes 100
  56.6 6.8 %copy-start.8 = (bf16[256,1024]{1,0:T(8,128)(2,1)S(1)}, bf16[256,1024]{1,0:T(8,128)(2,1)}, u32[]{:S(2)}) copy-start(bf16[256,1024]{1,0:T(8,128)(2,1)} %param.25) | copy-start | bytes 1572868
  56.6 100.5 %collective-permute-start.1 = (bf16[256,4096]{1,0:T(8,128)(2,1)}, bf16[256,4096]{1,0:T(8,128)(2,1)}, u32[]{:S(2)}, u32[]{:S(2)}) collective-permute-start(bf16[256,4096]{1,0:T(8,128)(2,1)} %pick_channels.5), channel_id=1, source_target_pairs={{0,1},{1,0},{2,3},{3,2},{4,5},{5,4},{6,7},{7,6},{8,9},{9,8},{10,11... | collective-permute-start | bytes 6291464 | tf_op jit(solution)/shard_map/ppermute | solution.py:658
  61.7 106.2 %collective-permute-start.7 = (bf16[256,4096]{1,0:T(8,128)(2,1)}, bf16[256,4096]{1,0:T(8,128)(2,1)}, u32[]{:S(2)}, u32[]{:S(2)}) collective-permute-start(bf16[256,4096]{1,0:T(8,128)(2,1)} %pick_channels.6), channel_id=1, source_target_pairs={{0,1},{1,0},{2,3},{3,2},{4,5},{5,4},{6,7},{7,6},{8,9},{9,8},{10,11... | collective-permute-start | bytes 6291464 | tf_op jit(solution)/shard_map/ppermute | solution.py:639
  61.8 12.6 %collective-permute-start.2 = (bf16[256,32]{0,1:T(8,128)(2,1)S(1)}, bf16[256,32]{0,1:T(8,128)(2,1)S(1)}, u32[]{:S(2)}, u32[]{:S(2)}) collective-permute-start(bf16[256,32]{0,1:T(8,128)(2,1)S(1)} %copy-done.15), channel_id=1, source_target_pairs={{0,1},{1,0},{2,3},{3,2},{4,5},{5,4},{6,7},{7,6},{8,9},{9,8},{10,11... | collective-permute-start | bytes 49160 | tf_op jit(solution)/shard_map/ppermute | solution.py:643
  73.8 80.2 %copy-start.4 = (bf16[256,512]{1,0:T(8,128)(2,1)S(1)}, bf16[256,512]{1,0:T(8,128)(2,1)}, u32[]{:S(2)}) copy-start(bf16[256,512]{1,0:T(8,128)(2,1)} %low_own_ref.1) | copy-start | bytes 786436
  74.5 80.1 %copy-start.16 = (bf16[256,32]{0,1:T(8,128)(2,1)}, bf16[256,32]{0,1:T(8,128)(2,1)S(1)}, u32[]{:S(2)}) copy-start(bf16[256,32]{0,1:T(8,128)(2,1)S(1)} %collective-permute-done.2) | copy-start | bytes 49156
  74.5 93.4 %collective-permute-start.8 = (bf16[256,4096]{1,0:T(8,128)(2,1)}, bf16[256,4096]{1,0:T(8,128)(2,1)}, u32[]{:S(2)}, u32[]{:S(2)}) collective-permute-start(bf16[256,4096]{1,0:T(8,128)(2,1)} %pick_channels.7), channel_id=1, source_target_pairs={{0,1},{1,0},{2,3},{3,2},{4,5},{5,4},{6,7},{7,6},{8,9},{9,8},{10,11... | collective-permute-start | bytes 6291464 | tf_op jit(solution)/shard_map/ppermute | solution.py:639
  86.2 182.5 %all-to-all-start.1 = ((bf16[256,8,256]{0,2,1:T(8,128)(2,1)}), bf16[256,8,256]{0,2,1:T(8,128)(2,1)S(1)}, u32[]{:S(2)}, u32[]{:S(2)}) async-start(bf16[256,8,256]{0,2,1:T(8,128)(2,1)} %bitcast.27), calls=%async_computation.1 | async-start | bytes 2097152 | tf_op jit(solution)/shard_map/all_to_all | solution.py:621
  89.8 57.5 %collective-permute-start.4 = (f32[24,2048]{1,0:T(8,128)}, f32[24,2048]{1,0:T(8,128)S(1)}, u32[]{:S(2)}, u32[]{:S(2)}) collective-permute-start(f32[24,2048]{1,0:T(8,128)} %concatenate.26), channel_id=1, source_target_pairs={{0,4},{2,6},{4,0},{6,2},{1,5},{3,7},{5,1},{7,3},{8,12},{10,14},{12... | collective-permute-start | bytes 589832 | tf_op jit(solution)/shard_map/ppermute | solution.py:662
  147.3 1.8 copy-start.12
  147.3 6.7 %collective-permute-start.5 = (f32[24,2048]{1,0:T(8,128)}, f32[24,2048]{1,0:T(8,128)}, u32[]{:S(2)}, u32[]{:S(2)}) collective-permute-start(f32[24,2048]{1,0:T(8,128)} %concatenate.26), channel_id=1, source_target_pairs={{0,6},{2,0},{4,2},{6,4},{1,7},{3,1},{5,3},{7,5},{8,14},{10,8},{12,... | collective-permute-start | bytes 589832 | tf_op jit(solution)/shard_map/ppermute | solution.py:662
  154.0 2.0 collective-permute-start.6
  156.0 11.9 %copy-start.5 = (bf16[256,512]{1,0:T(8,128)(2,1)}, bf16[256,512]{1,0:T(8,128)(2,1)S(1)}, u32[]{:S(2)}) copy-start(bf16[256,512]{1,0:T(8,128)(2,1)S(1)} %collective-permute-done.6.low_other_ref) | copy-start | bytes 786436
  156.0 26.1 %collective-permute-start.13 = (bf16[4,128,1024]{2,1,0:T(8,128)(2,1)S(1)}, bf16[4,128,1024]{2,1,0:T(8,128)(2,1)S(1)}, u32[]{:S(2)}, u32[]{:S(2)}) collective-permute-start(bf16[4,128,1024]{2,1,0:T(8,128)(2,1)S(1)} %pad_maximum_fusion.1.refs_0_), channel_id=1, source_target_pairs={{0,8},{8,0},{16,24},{24,16},{1,9},{9,1},{17,25},{25,17},{2,10},{10... | collective-permute-start | bytes 3145736 | tf_op jit(solution)/shard_map/ppermute | solution.py:618
  156.1 48.2 %collective-permute-start.14 = (bf16[4,128,1024]{2,1,0:T(8,128)(2,1)S(1)}, bf16[4,128,1024]{2,1,0:T(8,128)(2,1)}, u32[]{:S(2)}, u32[]{:S(2)}) collective-permute-start(bf16[4,128,1024]{2,1,0:T(8,128)(2,1)S(1)} %pad_maximum_fusion.1.refs_0_), channel_id=1, source_target_pairs={{0,16},{8,24},{16,0},{24,8},{1,17},{9,25},{17,1},{25,9},{2,18},{10... | collective-permute-start | bytes 3145736 | tf_op jit(solution)/shard_map/ppermute | solution.py:618
  157.1 47.2 %collective-permute-start.15 = (bf16[4,128,1024]{2,1,0:T(8,128)(2,1)S(1)}, bf16[4,128,1024]{2,1,0:T(8,128)(2,1)}, u32[]{:S(2)}, u32[]{:S(2)}) collective-permute-start(bf16[4,128,1024]{2,1,0:T(8,128)(2,1)S(1)} %pad_maximum_fusion.1.refs_0_), channel_id=1, source_target_pairs={{0,24},{8,16},{16,8},{24,0},{1,25},{9,17},{17,9},{25,1},{2,26},{10... | collective-permute-start | bytes 3145736 | tf_op jit(solution)/shard_map/ppermute | solution.py:618
  163.5 3.5 copy-start.10
  163.5 3.5 copy-start.11
  163.5 4.4 copy-start.13
  166.2 4.3 copy-start
  167.9 2.7 copy-start.7
  182.1 22.2 %copy-start.6 = (bf16[4,128,1024]{2,1,0:T(8,128)(2,1)}, bf16[4,128,1024]{2,1,0:T(8,128)(2,1)S(1)}, u32[]{:S(2)}) copy-start(bf16[4,128,1024]{2,1,0:T(8,128)(2,1)S(1)} %collective-permute-done.13.refs_1_) | copy-start | bytes 3145732
  269.2 10.4 %copy-start.3 = (bf16[8,256,256]{2,1,0:T(8,128)(2,1)}, bf16[8,256,256]{2,1,0:T(8,128)(2,1)S(1)}, u32[]{:S(2)}) copy-start(bf16[8,256,256]{2,1,0:T(8,128)(2,1)S(1)} %copy.40) | copy-start | bytes 3145732
  272.7 74.5 %all-to-all-start.2 = ((bf16[256,8,512]{2,0,1:T(8,128)(2,1)}), bf16[256,8,512]{2,0,1:T(8,128)(2,1)S(1)}, u32[]{:S(2)}, u32[]{:S(2)}) async-start(bf16[256,8,512]{2,0,1:T(8,128)(2,1)} %bitcast.57), calls=%async_computation.2 | async-start | bytes 4194304 | tf_op jit(solution)/shard_map/all_to_all | solution.py:705
  277.6 76.6 %collective-permute-start.16 = (bf16[2048,256]{1,0:T(8,128)(2,1)S(1)}, bf16[2048,256]{1,0:T(8,128)(2,1)}, u32[]{:S(2)}, u32[]{:S(2)}) collective-permute-start(bf16[2048,256]{1,0:T(8,128)(2,1)S(1)} %bitcast.58), channel_id=1, source_target_pairs={{0,8},{8,0},{16,24},{24,16},{1,9},{9,1},{17,25},{25,17},{2,10},{10... | collective-permute-start | bytes 3145736 | tf_op jit(solution)/shard_map/ppermute | solution.py:706
  279.2 75.0 %collective-permute-start.17 = (bf16[2048,256]{1,0:T(8,128)(2,1)S(1)}, bf16[2048,256]{1,0:T(8,128)(2,1)}, u32[]{:S(2)}, u32[]{:S(2)}) collective-permute-start(bf16[2048,256]{1,0:T(8,128)(2,1)S(1)} %bitcast.59), channel_id=1, source_target_pairs={{0,16},{8,24},{16,0},{24,8},{1,17},{9,25},{17,1},{25,9},{2,18},{10... | collective-permute-start | bytes 3145736 | tf_op jit(solution)/shard_map/ppermute | solution.py:706
  279.6 74.6 %collective-permute-start.18 = (bf16[2048,256]{1,0:T(8,128)(2,1)S(1)}, bf16[2048,256]{1,0:T(8,128)(2,1)}, u32[]{:S(2)}, u32[]{:S(2)}) collective-permute-start(bf16[2048,256]{1,0:T(8,128)(2,1)S(1)} %bitcast.60), channel_id=1, source_target_pairs={{0,24},{8,16},{16,8},{24,0},{1,25},{9,17},{17,9},{25,1},{2,26},{10... | collective-permute-start | bytes 3145736 | tf_op jit(solution)/shard_map/ppermute | solution.py:706
  281.1 64.3 %copy-start.9 = (bf16[16,32,256]{2,1,0:T(8,128)(2,1)S(1)}, bf16[16,32,256]{2,1,0:T(8,128)(2,1)}, u32[]{:S(2)}) copy-start(bf16[16,32,256]{2,1,0:T(8,128)(2,1)} %get-tuple-element.58) | copy-start | bytes 786436
  345.4 8.2 %copy-start.14 = (f32[16,256]{1,0:T(8,128)S(1)}, f32[16,256]{1,0:T(8,128)}, u32[]{:S(2)}) copy-start(f32[16,256]{1,0:T(8,128)} %get-tuple-element.73) | copy-start | bytes 49156
  347.2 7.0 %copy-start.1 = (bf16[256,8,512]{2,0,1:T(8,128)(2,1)}, bf16[256,8,512]{2,0,1:T(8,128)(2,1)S(1)}, u32[]{:S(2)}) copy-start(bf16[256,8,512]{2,0,1:T(8,128)(2,1)S(1)} %all-to-all-done.2) | copy-start | bytes 6291460
  347.2 65.2 %all-to-all-start.3 = ((bf16[16,32,512]{2,1,0:T(8,128)(2,1)}), bf16[16,32,512]{2,1,0:T(8,128)(2,1)}, u32[]{:S(2)}, u32[]{:S(2)}) async-start(bf16[16,32,512]{2,1,0:T(8,128)(2,1)} %pad_maximum_fusion.3), calls=%async_computation.3 | async-start | bytes 1048576 | tf_op jit(solution)/shard_map/all_to_all | solution.py:684
  431.5 97.4 %all-to-all-start.5 = ((bf16[8,256,512]{2,1,0:T(8,128)(2,1)}), bf16[8,256,512]{2,1,0:T(8,128)(2,1)S(1)}, u32[]{:S(2)}, u32[]{:S(2)}) async-start(bf16[8,256,512]{2,1,0:T(8,128)(2,1)} %bitcast.54), calls=%async_computation.5 | async-start | bytes 4194304 | tf_op jit(solution)/shard_map/all_to_all | solution.py:716
  477.6 42.3 %collective-permute-start.19 = (bf16[256,4096]{1,0:T(8,128)(2,1)}, bf16[256,4096]{1,0:T(8,128)(2,1)}, u32[]{:S(2)}, u32[]{:S(2)}) collective-permute-start(bf16[256,4096]{1,0:T(8,128)(2,1)} %get-tuple-element.83), channel_id=1, source_target_pairs={{0,1},{1,0},{2,3},{3,2},{4,5},{5,4},{6,7},{7,6},{8,9},{9,8},{10,11... | collective-permute-start | bytes 6291464 | tf_op jit(solution)/shard_map/ppermute | solution.py:718
  519.8 4.6 collective-permute-start.20
Sparse Core Ops, SparseCore 0:
  32.9 114.0 all-gather.2
